TPU v7x, 128 devices: a whole 4x4x4 slice. The times are simulated.
128 devices in a mesh: slide: 4 (over x), gy: 8 (over z_lo, y), gx: 4 (over z_hi, core).
Axes of the slice: x: 4, y: 4, z: 4 (z_hi: 2, z_lo: 2; z = z_hi * 2 + z_lo), core: 2. Of those that a mesh axis runs over, the one named last changes fastest.
Arguments:
- tokens: bfloat16 [4, 128, 64, 1024], P('slide', 'gy', 'gx'), may hold values from -64 to 64, as said below
- weights: bfloat16 [1024, 4096], replicated, may hold values from -5 to 5
- norm_gain: float32 [1024], replicated, may hold values from 0.25 to 1.75
- tissue: int32 [4, 128, 64], P('slide', 'gy', 'gx'), may hold values from 0 to 1, as said below
- cotangent: bfloat16 [4, 128, 64, 1024], P('slide', 'gy', 'gx'), may hold values from -6 to 6
Outputs:
- block_output: bfloat16 [4, 128, 64, 1024], P('slide', 'gy', 'gx')
- input_grad: bfloat16 [4, 128, 64, 1024], P('slide', 'gy', 'gx')
- weight_grads: float32 [1024, 4096], P(('slide', 'gy', 'gx'))
Inputs may be any that keep to these rules, and one draw needn't show every extreme that they name: `tokens`: token activations. 1 marks a tissue token, 0 background.
All inputs are finite; a program needn't handle non-finite values.
Results may differ from a plain program's by a relative error of at most 0.015.
The roundings to bfloat16 on the way count: a program that leaves them out, or rounds other values in their place, can miss the bound.
Values may be sent and summed in bfloat16 or wider, within the bound.
A program may use at most 128 MiB of HBM per device.

v0:
```python
import math

import jax
import jax.numpy as jnp
from jax import lax
from jax.sharding import PartitionSpec as P

HEADS = 16
RADIUS = 6


EPSILON = 1e-06


def with_halo(block, sides, width):
    for axis, dim in sides:
        count = lax.axis_size(axis)
        forward = [(i, i + 1) for i in range(count - 1)]
        backward = [(target, source) for source, target in forward]
        low = lax.ppermute(
            lax.slice_in_dim(block, block.shape[dim] - width, None, axis=dim), axis, forward
        )
        high = lax.ppermute(lax.slice_in_dim(block, 0, width, axis=dim), axis, backward)
        block = jnp.concatenate([low, block, high], axis=dim)
    return block


def shifted(shard, axis, by):
    count = lax.axis_size(axis)
    pairs = [(i, i + by) for i in range(count) if 0 <= i + by < count]
    return lax.ppermute(shard, axis, pairs)


def contract(pattern, left_operand, second):
    return jnp.einsum(pattern, left_operand, second, preferred_element_type=jnp.float32)


def into_blocks(array, blocks_down, blocks_across, head_dim):
    shaped = array.reshape(blocks_down, 8, blocks_across, 8, HEADS, head_dim)
    return shaped.transpose(0, 2, 1, 3, 4, 5).reshape(
        blocks_down * blocks_across, 64, HEADS, head_dim
    )


def from_blocks(array, blocks_down, blocks_across):
    model_width = array.shape[2] * array.shape[3]
    shaped = array.reshape(blocks_down, blocks_across, 8, 8, model_width)
    return shaped.transpose(0, 2, 1, 3, 4).reshape(blocks_down * 8, blocks_across * 8, model_width)


def stack_windows(array, blocks_count):
    return jnp.stack([array[offset : offset + blocks_count] for offset in range(3)], axis=1)


def tile_attention(queries, key_values, grad_attn, row_valid, col_valid):
    tile_rows, tile_cols, model_width = queries.shape
    head_dim = model_width // HEADS
    blocks_down = tile_rows // 8
    blocks_across = tile_cols // 8
    block_count = blocks_down * blocks_across
    window_edge = 8 + 2 * RADIUS
    window_size = window_edge * window_edge
    extra_rows = 16 - 2 * RADIUS
    channels = key_values.shape[2]
    padded = jnp.pad(key_values, ((0, extra_rows), (0, extra_rows), (0, 0)))
    block_grid = padded.reshape(blocks_down + 2, 8, blocks_across + 2, 8, channels)
    row_stack = stack_windows(block_grid, blocks_down)
    full_stack = jnp.stack(
        [row_stack[:, :, :, offset : offset + blocks_across] for offset in range(3)], axis=4
    )
    windows = full_stack.reshape(blocks_down, 24, blocks_across, 24, channels)[
        :, :window_edge, :, :window_edge
    ]
    windows = windows.transpose(0, 2, 1, 3, 4).reshape(block_count, window_size, channels)
    row_padded = jnp.pad(row_valid, (0, extra_rows)).reshape(blocks_down + 2, 8)
    row_window = stack_windows(row_padded, blocks_down).reshape(blocks_down, 24)[:, :window_edge]
    col_padded = jnp.pad(col_valid, (0, extra_rows)).reshape(blocks_across + 2, 8)
    col_window = stack_windows(col_padded, blocks_across).reshape(blocks_across, 24)[
        :, :window_edge
    ]
    query_slot = jnp.arange(64)
    key_slot = jnp.arange(window_size)
    query_row = (query_slot // 8)[:, None]
    query_col = (query_slot % 8)[:, None]
    key_row = (key_slot // window_edge)[None, :]
    key_col = (key_slot % window_edge)[None, :]
    nearby = (key_row >= query_row) & (key_row <= query_row + 2 * RADIUS)
    nearby = nearby & (key_col >= query_col) & (key_col <= query_col + 2 * RADIUS)
    in_grid = (row_window[:, None, :, None] & col_window[None, :, None, :]).reshape(
        block_count, 1, 1, window_size
    )
    allowed = nearby[None, None] & in_grid
    query_blocks = into_blocks(queries, blocks_down, blocks_across, head_dim)
    grad_blocks = into_blocks(grad_attn, blocks_down, blocks_across, head_dim)
    key_blocks = windows[:, :, :model_width].reshape(block_count, window_size, HEADS, head_dim)
    value_blocks = windows[:, :, model_width:].reshape(block_count, window_size, HEADS, head_dim)
    scaling = 1.0 / math.sqrt(head_dim)
    scores = contract("nqhd,nkhd->nhqk", query_blocks, key_blocks) * scaling
    scores = jnp.where(allowed, scores, -1e30)
    row_max = jnp.max(scores, axis=-1, keepdims=True)
    exponent = jnp.exp(scores - row_max)
    attn_probs = exponent / jnp.sum(exponent, axis=-1, keepdims=True)
    probs_bf = attn_probs.astype(jnp.bfloat16)
    attended = contract("nhqk,nkhd->nqhd", probs_bf, value_blocks).astype(jnp.bfloat16)
    grad_probs = contract("nqhd,nkhd->nhqk", grad_blocks, value_blocks)
    centred = grad_probs - jnp.sum(attn_probs * grad_probs, axis=-1, keepdims=True)
    grad_scores = (attn_probs * centred * scaling).astype(jnp.bfloat16)
    grad_queries = contract("nhqk,nkhd->nqhd", grad_scores, key_blocks).astype(jnp.bfloat16)
    grad_keys = contract("nhqk,nqhd->nkhd", grad_scores, query_blocks)
    grad_values = contract("nhqk,nqhd->nkhd", probs_bf, grad_blocks)
    grad_windows = jnp.concatenate(
        [
            grad_keys.reshape(block_count, window_size, model_width),
            grad_values.reshape(block_count, window_size, model_width),
        ],
        axis=-1,
    )
    grad_windows = grad_windows.reshape(
        blocks_down, blocks_across, window_edge, window_edge, channels
    )
    grad_windows = jnp.pad(
        grad_windows, ((0, 0), (0, 0), (0, 24 - window_edge), (0, 24 - window_edge), (0, 0))
    )
    grad_windows = grad_windows.reshape(blocks_down, blocks_across, 3, 8, 3, 8, channels)
    accumulated = jnp.zeros((blocks_down + 2, 8, blocks_across + 2, 8, channels), jnp.float32)
    for offset_down in range(3):
        for offset_across in range(3):
            window_part = grad_windows[:, :, offset_down, :, offset_across].transpose(0, 2, 1, 3, 4)
            accumulated = accumulated.at[
                offset_down : offset_down + blocks_down,
                :,
                offset_across : offset_across + blocks_across,
            ].add(window_part)
    accumulated = accumulated.reshape(8 * (blocks_down + 2), 8 * (blocks_across + 2), channels)
    accumulated = accumulated[: tile_rows + 2 * RADIUS, : tile_cols + 2 * RADIUS]
    return (
        from_blocks(attended, blocks_down, blocks_across),
        from_blocks(grad_queries, blocks_down, blocks_across),
        accumulated,
    )


def run_strips(queries, padded_kv, grad_attn, row_valid, col_valid):
    tile_rows, tile_cols, model_width = queries.shape

    def strip_step(strip_index, carry):
        attended_all, grad_query_all, grad_padded_all = carry
        top_row = (strip_index * 8).astype(jnp.int32)
        query_strip = lax.dynamic_slice_in_dim(queries, top_row, 8, 0)
        kv_strip = lax.dynamic_slice_in_dim(padded_kv, top_row, 8 + 2 * RADIUS, 0)
        grad_strip = lax.dynamic_slice_in_dim(grad_attn, top_row, 8, 0)
        valid_strip = lax.dynamic_slice_in_dim(row_valid, top_row, 8 + 2 * RADIUS, 0)
        attended, grad_queries, grad_padded = tile_attention(
            query_strip, kv_strip, grad_strip, valid_strip, col_valid
        )
        attended_all = lax.dynamic_update_slice_in_dim(attended_all, attended, top_row, 0)
        grad_query_all = lax.dynamic_update_slice_in_dim(grad_query_all, grad_queries, top_row, 0)
        previous = lax.dynamic_slice_in_dim(grad_padded_all, top_row, 8 + 2 * RADIUS, 0)
        grad_padded_all = lax.dynamic_update_slice_in_dim(
            grad_padded_all, previous + grad_padded, top_row, 0
        )
        return (attended_all, grad_query_all, grad_padded_all)

    start_carry = (
        jnp.zeros((tile_rows, tile_cols, model_width), jnp.bfloat16),
        jnp.zeros((tile_rows, tile_cols, model_width), jnp.bfloat16),
        jnp.zeros((tile_rows + 2 * RADIUS, tile_cols + 2 * RADIUS, 2 * model_width), jnp.float32),
    )
    return lax.fori_loop(0, tile_rows // 8, strip_step, start_carry)


def local(tokens, weights, norm_gain, tissue, cotangent):
    tile_tokens = tokens[0]
    tile_rows, tile_cols, model_width = tile_tokens.shape
    token_count = tile_rows * tile_cols
    group_count = lax.axis_size("slide") * lax.axis_size("gy") * lax.axis_size("gx")
    weight_in = weights[:, : 3 * model_width]
    weight_out = weights[:, 3 * model_width :]
    tokens_float = tile_tokens.astype(jnp.float32)
    row_mean = jnp.mean(tokens_float, axis=-1, keepdims=True)
    centered = tokens_float - row_mean
    variance = jnp.mean(centered * centered, axis=-1, keepdims=True)
    inverse = lax.rsqrt(variance + EPSILON)
    normalized = centered * inverse
    normed = (normalized * norm_gain).astype(jnp.bfloat16)
    normed_flat = normed.reshape(token_count, model_width)
    projected = jnp.dot(normed_flat, weight_in, preferred_element_type=jnp.float32).astype(
        jnp.bfloat16
    )
    projected = projected.reshape(tile_rows, tile_cols, 3 * model_width)
    queries = projected[:, :, :model_width]
    key_values = projected[:, :, model_width:]
    tissue_tile = tissue[0]
    tissue_mask = tissue_tile.astype(jnp.float32)[:, :, None]
    upstream = cotangent[0].astype(jnp.float32)
    branch_grad = (tissue_mask * upstream).astype(jnp.bfloat16)
    branch_flat = branch_grad.reshape(token_count, model_width)
    grad_attn = jnp.dot(branch_flat, weight_out.T, preferred_element_type=jnp.float32).astype(
        jnp.bfloat16
    )
    grad_attn = grad_attn.reshape(tile_rows, tile_cols, model_width)
    padded_kv = with_halo(key_values, (("gy", 0), ("gx", 1)), RADIUS)
    row_coord = jnp.arange(tile_rows + 2 * RADIUS) + lax.axis_index("gy") * tile_rows - RADIUS
    row_valid = (row_coord >= 0) & (row_coord < tile_rows * lax.axis_size("gy"))
    col_coord = jnp.arange(tile_cols + 2 * RADIUS) + lax.axis_index("gx") * tile_cols - RADIUS
    col_valid = (col_coord >= 0) & (col_coord < tile_cols * lax.axis_size("gx"))
    operands = (queries, padded_kv, grad_attn, row_valid, col_valid)
    attended, grad_queries, grad_padded = run_strips(*operands)
    attended_flat = attended.reshape(token_count, model_width)
    inv_root = 1.0 / math.sqrt(group_count * token_count)
    projection = jnp.dot(attended_flat, weight_out, preferred_element_type=jnp.float32)
    block_output = (
        tokens_float + tissue_mask * projection.reshape(tile_rows, tile_cols, model_width)
    ).astype(jnp.bfloat16)
    column_fold = grad_padded[:, RADIUS : RADIUS + tile_cols]
    for shift_by, rim_part in (
        (-1, grad_padded[:, :RADIUS]),
        (1, grad_padded[:, RADIUS + tile_cols :]),
    ):
        arrived = shifted(rim_part.astype(jnp.bfloat16), "gx", shift_by).astype(rim_part.dtype)
        if shift_by < 0:
            column_fold = column_fold.at[:, tile_cols - RADIUS :].add(arrived)
        else:
            column_fold = column_fold.at[:, :RADIUS].add(arrived)
    row_fold = column_fold[RADIUS : RADIUS + tile_rows]
    for shift_by, rim_part in ((-1, column_fold[:RADIUS]), (1, column_fold[RADIUS + tile_rows :])):
        arrived = shifted(rim_part.astype(jnp.bfloat16), "gy", shift_by).astype(rim_part.dtype)
        if shift_by < 0:
            row_fold = row_fold.at[tile_rows - RADIUS :].add(arrived)
        else:
            row_fold = row_fold.at[:RADIUS].add(arrived)
    grad_kv = row_fold.astype(jnp.bfloat16)
    grad_projected = jnp.concatenate([grad_queries, grad_kv], axis=-1).reshape(
        token_count, 3 * model_width
    )
    grad_normed = jnp.dot(grad_projected, weight_in.T, preferred_element_type=jnp.float32)
    grad_normed = grad_normed.reshape(tile_rows, tile_cols, model_width)
    scaled = grad_normed * norm_gain
    first_mean = jnp.mean(scaled, axis=-1, keepdims=True)
    second_mean = jnp.mean(scaled * normalized, axis=-1, keepdims=True)
    input_grad = (upstream + inverse * (scaled - first_mean - normalized * second_mean)).astype(
        jnp.bfloat16
    )
    weight_grads = lax.psum_scatter(
        jnp.concatenate(
            [
                lax.dot_general(
                    normed_flat,
                    grad_projected,
                    (((0,), (0,)), ((), ())),
                    preferred_element_type=jnp.float32,
                )
                * inv_root,
                lax.dot_general(
                    attended_flat,
                    branch_flat,
                    (((0,), (0,)), ((), ())),
                    preferred_element_type=jnp.float32,
                )
                * inv_root,
            ],
            axis=1,
        ),
        ("slide", "gy", "gx"),
        scatter_dimension=0,
        tiled=True,
    )
    return (block_output[None], input_grad[None], weight_grads)


def solution(mesh):
    in_specs = (
        P("slide", "gy", "gx", None),
        P(),
        P(),
        P("slide", "gy", "gx"),
        P("slide", "gy", "gx", None),
    )
    out_specs = (
        P("slide", "gy", "gx", None),
        P("slide", "gy", "gx", None),
        P(("slide", "gy", "gx"), None),
    )
    return jax.shard_map(local, mesh=mesh, in_specs=in_specs, out_specs=out_specs, check_vma=False)
```

profile of v0, /device:TPU:1, one launch (start us, length us, event | category | flops | bytes accessed | tf_op | source)
XLA Modules:
  0.0 1127.8 jit_solution(4365566473644824217)
XLA Ops:
  11.3 4.6 fusion.75
  17.7 4.8 collective-permute-start
  23.2 8.3 collective-permute-done.1
  34.5 7.4 collective-permute-start.2
  44.8 2.3 fusion.95
  47.1 4.0 collective-permute-done.2
  51.2 5.9 collective-permute-done.3
  57.1 2.4 pad_maximum_fusion.4
  59.5 3.7 copy.103
  64.8 3.9 broadcast_in_dim.81
  68.7 311.2 %while.33 = (s32[]{:T(128)}, bf16[16,16,1024]{2,1,0:T(8,128)(2,1)}, bf16[16,16,1024]{2,1,0:T(8,128)(2,1)}, f32[28,28,2048]{2,1,0:T(8,128)}, bf16[28,28,2048]{2,1...) while((s32[]{:T(128)}, bf16[16,16,1024]{2,1,0:T(8,128)(2,1)}, ...), condition=%wide.region_8.9_spmd, body=%wide.region_2.8_spmd.sunk | while | flops 662583808 | bytes 314590624 | solution.py:169
  97.8 2.1 constant_dynamic-slice_fusion.6
  102.1 3.4 copy.166
  105.5 3.5 fusion.196
  109.1 4.6 copy.167
  113.7 6.0 copy.168
  119.7 2.7 fusion.202
  123.1 3.6 fusion.200
  126.7 18.6 %fusion.203 = bf16[2,64,16,64]{1,3,2,0:T(8,128)(2,1)} fusion(bf16[2,400,16,64]{1,3,2,0:T(8,128)(2,1)} %bitcast.350, f32[2,16,64,400]{3,2,1,0:T(8,128)} %fusion.202, f32[2,16,64,400]{3,2,1,0:T(8,128)} %get-tuple-element.709, f32[2,16,64]{2,1,0:T(8,128)S(1)} %get-tuple-element.710), kind=kOutput, calls=%fused_computation.36.clone.1 | convolution fusion | flops 110725520 | bytes 8462336 | tf_op jit(solution)/shard_map/while/body/eval_jaxpr/nhqk,nkhd->nqhd/dot_general | solution.py:35
  145.3 3.8 fusion.201
  149.1 18.6 %fusion.204 = f32[2,400,16,64]{1,3,2,0:T(8,128)} fusion(f32[2,16,64,400]{3,2,1,0:T(8,128)} %fusion.202, bf16[1,2,8,8,16,64]{5,4,3,1,2,0:T(8,128)(2,1)S(1)} %bitcast.355, f32[2,16,64,400]{3,2,1,0:T(8,128)} %get-tuple-element.709, f32[2,16,64]{2,1,0:T(8,128)S(1)} %get-tuple-element.710), kind=kOutput, calls=%fused_computation.20.clone.1 | convolution fusion | flops 110594448 | bytes 10100736 | tf_op jit(solution)/shard_map/while/body/eval_jaxpr/nhqk,nqhd->nkhd/dot_general | solution.py:35
  167.7 5.1 convolution_bitcast_fusion.2
  176.0 6.4 copy.172
  182.4 5.8 concatenate.124
  188.2 6.4 copy.173
  194.6 7.1 concatenate.125
  201.7 9.0 pad_maximum_fusion.16
  210.7 6.7 copy.174
  221.3 2.1 fusion.207
  229.4 2.9 copy-done
  238.3 2.1 constant_dynamic-slice_fusion.6
  242.5 3.4 copy.166
  246.0 3.5 fusion.196
  249.5 4.6 copy.167
  254.1 6.0 copy.168
  260.2 2.7 fusion.202
  263.5 3.6 fusion.200
  267.1 18.6 %fusion.203 = bf16[2,64,16,64]{1,3,2,0:T(8,128)(2,1)} fusion(bf16[2,400,16,64]{1,3,2,0:T(8,128)(2,1)} %bitcast.350, f32[2,16,64,400]{3,2,1,0:T(8,128)} %fusion.202, f32[2,16,64,400]{3,2,1,0:T(8,128)} %get-tuple-element.709, f32[2,16,64]{2,1,0:T(8,128)S(1)} %get-tuple-element.710), kind=kOutput, calls=%fused_computation.36.clone.1 | convolution fusion | flops 110725520 | bytes 8462336 | tf_op jit(solution)/shard_map/while/body/eval_jaxpr/nhqk,nkhd->nqhd/dot_general | solution.py:35
  285.8 3.8 fusion.201
  289.5 18.6 %fusion.204 = f32[2,400,16,64]{1,3,2,0:T(8,128)} fusion(f32[2,16,64,400]{3,2,1,0:T(8,128)} %fusion.202, bf16[1,2,8,8,16,64]{5,4,3,1,2,0:T(8,128)(2,1)S(1)} %bitcast.355, f32[2,16,64,400]{3,2,1,0:T(8,128)} %get-tuple-element.709, f32[2,16,64]{2,1,0:T(8,128)S(1)} %get-tuple-element.710), kind=kOutput, calls=%fused_computation.20.clone.1 | convolution fusion | flops 110594448 | bytes 10100736 | tf_op jit(solution)/shard_map/while/body/eval_jaxpr/nhqk,nqhd->nkhd/dot_general | solution.py:35
  308.2 5.1 convolution_bitcast_fusion.2
  316.4 6.4 copy.172
  322.8 5.8 concatenate.124
  328.7 6.4 copy.173
  335.1 7.1 concatenate.125
  342.2 9.0 pad_maximum_fusion.16
  351.1 6.7 copy.174
  361.8 2.1 fusion.207
  369.8 2.9 copy-done
  379.9 6.7 copy.145
  388.6 5.1 collective-permute-start.5
  393.8 2.6 slice.1180
  396.4 5.1 collective-permute-done.4
  402.0 8.5 scatter-add.44
  410.5 2.0 slice_add_fusion.1
  412.5 9.3 scatter-add.54
  421.9 2.4 convert.12
  428.0 4.9 collective-permute-start.7
  433.7 3.9 collective-permute-done.7
  437.9 2.0 bitcast_multiply_fusion
  439.9 6.2 pad_maximum_fusion.3
  446.2 3.1 fusion.98
  449.3 4.8 fusion.129
  455.3 665.4 %reduce-scatter.2.cloned.1.call-done = f32[8,4096]{1,0:T(8,128)} async-done(((f32[1024,4096]{1,0:T(8,128)}), f32[8,4096]{1,0:T(8,128)}) %reduce-scatter.2.cloned.1.call-update) | async-done | bytes 131088 | tf_op jit(solution)/shard_map/reduce_scatter | solution.py:244
  (238 shorter events, 65.8 us)
Async XLA Ops:
  7.2 1113.5 %reduce-scatter.2.cloned.1.call-start = ((), (), s32[]{:S(2)}) async-start(), calls=%async_computation.1 | async-start | bytes 16908288 | tf_op jit(solution)/shard_map/reduce_scatter | solution.py:244
  8.4 7.4 copy-start.17
  9.8 6.0 copy-start.19
  16.2 15.3 %collective-permute-start.1 = (bf16[6,16,2048]{2,0,1:T(8,128)(2,1)S(1)}, bf16[6,16,2048]{2,0,1:T(8,128)(2,1)S(1)}, u32[]{:S(2)}, u32[]{:S(2)}) collective-permute-start(bf16[6,16,2048]{2,0,1:T(8,128)(2,1)S(1)} %copy.123), channel_id=1, source_target_pairs={{4,0},{8,4},{12,8},{16,12},{20,16},{24,20},{28,24},{5,1},{9,5},{13... | collective-permute-start | bytes 1179656 | tf_op jit(solution)/shard_map/ppermute | solution.py:23
  17.5 26.4 %copy-start.22 = (s32[1,16,16]{2,1,0:T(8,128)S(1)}, s32[1,16,16]{2,1,0:T(8,128)}, u32[]{:S(2)}) copy-start(s32[1,16,16]{2,1,0:T(8,128)} %param.36) | copy-start | bytes 3076
  17.7 26.9 %copy-start.11 = (bf16[1,16,16,1024]{3,2,1,0:T(8,128)(2,1)S(1)}, bf16[1,16,16,1024]{3,2,1,0:T(8,128)(2,1)}, u32[]{:S(2)}) copy-start(bf16[1,16,16,1024]{3,2,1,0:T(8,128)(2,1)} %param.37) | copy-start | bytes 1572868
  17.7 15.0 %collective-permute-start = (bf16[6,16,2048]{2,0,1:T(8,128)(2,1)S(1)}, bf16[6,16,2048]{2,0,1:T(8,128)(2,1)S(1)}, u32[]{:S(2)}, u32[]{:S(2)}) collective-permute-start(bf16[6,16,2048]{2,0,1:T(8,128)(2,1)S(1)} %copy.121), channel_id=1, source_target_pairs={{0,4},{4,8},{8,12},{12,16},{16,20},{20,24},{24,28},{1,5},{5,9},{9,... | collective-permute-start | bytes 1179656 | tf_op jit(solution)/shard_map/ppermute | solution.py:20
  34.5 16.6 %collective-permute-start.2 = (bf16[28,6,2048]{2,0,1:T(8,128)(2,1)}, bf16[28,6,2048]{2,0,1:T(8,128)(2,1)}, u32[]{:S(2)}, u32[]{:S(2)}) collective-permute-start(bf16[28,6,2048]{2,0,1:T(8,128)(2,1)} %get-tuple-element.607), channel_id=1, source_target_pairs={{0,1},{1,2},{2,3},{4,5},{5,6},{6,7},{8,9},{9,10},{10,11},{12,13},{... | collective-permute-start | bytes 2064392 | tf_op jit(solution)/shard_map/ppermute | solution.py:20
  42.0 15.1 %collective-permute-start.3 = (bf16[28,6,2048]{2,0,1:T(8,128)(2,1)}, bf16[28,6,2048]{2,0,1:T(8,128)(2,1)}, u32[]{:S(2)}, u32[]{:S(2)}) collective-permute-start(bf16[28,6,2048]{2,0,1:T(8,128)(2,1)} %get-tuple-element.608), channel_id=1, source_target_pairs={{1,0},{2,1},{3,2},{5,4},{6,5},{7,6},{9,8},{10,9},{11,10},{13,12},{... | collective-permute-start | bytes 2064392 | tf_op jit(solution)/shard_map/ppermute | solution.py:23
  63.1 5.6 copy-start.21
  91.8 8.5 copy-start.7
  91.8 8.5 copy-start.9
  119.7 2.7 copy-start.2
  167.7 5.2 copy-start.5
  167.7 5.9 copy-start.4
  167.7 6.7 copy-start.13
  175.2 0.8 copy-start.14
  224.7 1.9 slice-start
  225.0 2.9 slice-start.1
  228.0 4.4 copy-start.8
  228.0 4.4 copy-start.10
  229.4 2.9 copy-start
  232.3 8.5 copy-start.7
  232.3 8.5 copy-start.9
  260.2 2.7 copy-start.2
  308.1 5.2 copy-start.5
  308.1 5.9 copy-start.4
  308.1 6.7 copy-start.13
  315.6 0.8 copy-start.14
  365.2 1.9 slice-start
  365.5 2.9 slice-start.1
  368.4 4.4 copy-start.8
  368.4 4.4 copy-start.10
  369.8 2.9 copy-start
  379.9 13.9 %copy-start.1 = (f32[28,28,2048]{2,1,0:T(8,128)S(1)}, f32[28,28,2048]{2,1,0:T(8,128)}, u32[]{:S(2)}) copy-start(f32[28,28,2048]{2,1,0:T(8,128)} %get-tuple-element.553) | copy-start | bytes 19267588
  386.7 14.8 %collective-permute-start.4 = (bf16[28,6,2048]{2,0,1:T(8,128)(2,1)S(1)}, bf16[28,6,2048]{2,0,1:T(8,128)(2,1)S(1)}, u32[]{:S(2)}, u32[]{:S(2)}) collective-permute-start(bf16[28,6,2048]{2,0,1:T(8,128)(2,1)S(1)} %get-tuple-element.606), channel_id=1, source_target_pairs={{1,0},{2,1},{3,2},{5,4},{6,5},{7,6},{9,8},{10,9},{11,10},{13,12},{... | collective-permute-start | bytes 2064392 | tf_op jit(solution)/shard_map/ppermute | solution.py:31
  388.6 21.9 %collective-permute-start.5 = (bf16[28,6,2048]{2,0,1:T(8,128)(2,1)S(1)}, bf16[28,6,2048]{2,0,1:T(8,128)(2,1)S(1)}, u32[]{:S(2)}, u32[]{:S(2)}) collective-permute-start(bf16[28,6,2048]{2,0,1:T(8,128)(2,1)S(1)} %get-tuple-element.605), channel_id=1, source_target_pairs={{0,1},{1,2},{2,3},{4,5},{5,6},{6,7},{8,9},{9,10},{10,11},{12,13},{... | collective-permute-start | bytes 2064392 | tf_op jit(solution)/shard_map/ppermute | solution.py:31
  421.9 3.8 copy-start.12
  421.9 3.8 copy-start.16
  421.9 3.8 copy-start.23
  424.3 9.3 collective-permute-start.6
  425.6 2.0 copy-start.3
  427.9 10.0 copy-start.6
  427.9 10.0 copy-start.15
  427.9 10.0 copy-start.18
  427.9 10.0 copy-start.20
  428.0 10.0 copy-start.24
  428.0 9.6 collective-permute-start.7
Sparse Core Ops, SparseCore 0:
  446.3 674.3 reduce-scatter.1
where the time goes:
time: 1140 us; the launch traced here: 1130 us
  waiting for transfers between devices  695 us (61%)
  local copies, waits for them, and re-layouts  179 us (16%)
  matrix products  117 us (10%)
  other arithmetic  63.1 us (6%)
  loops' own time  31 us (3%)
  starting transfers between devices  28.7 us (3%)
  between operations  14.7 us (1%)
    reduce_scatter x1, waiting for transfers between devices, local(): lax.psum_scatter(jnp.concatenate([lax.dot_general(normed_flat, grad_proje...  665 us
    dot_general x12, matrix products, contract(): jnp.einsum(pattern, left_operand, second, preferred_element_type=jnp.floa...  99.1 us
    another operation x1, loops' own time, run_strips(): return lax.fori_loop(0, tile_rows // 8, strip_step, start_carry)  31 us
    while x50, local copies, waits for them, and re-layouts  25.9 us
    concatenate x4, local copies, waits for them, and re-layouts, tile_attention(): jnp.concatenate([grad_keys.reshape(block_count, window_size, model_width)...  25.9 us
    transpose x4, local copies, waits for them, and re-layouts, contract(): jnp.einsum(pattern, left_operand, second, preferred_element_type=jnp.floa...  25.6 us
  transfers between devices with their start and end apart: 9, of which 8 were waited for; matrix products, arithmetic and copies ran while one was open for 2% of the time, Pallas kernels for 0%

commit v1 on v0

--- a/solution.py
+++ b/solution.py
@@ -1,8 +1,11 @@
+import functools
 import math
 
 import jax
 import jax.numpy as jnp
 from jax import lax
+from jax.experimental import pallas as pl
+from jax.experimental.pallas import tpu as pltpu
 from jax.sharding import PartitionSpec as P
 
 HEADS = 16
@@ -167,6 +170,255 @@
         jnp.zeros((tile_rows + 2 * RADIUS, tile_cols + 2 * RADIUS, 2 * model_width), jnp.float32),
     )
     return lax.fori_loop(0, tile_rows // 8, strip_step, start_carry)
+
+
+COLOR_COLS = ((0, 768), (768, 768), (1536, 512))
+COLOR_AXES = ("xyz", "yzx", "zxy")
+
+
+def coords():
+    x = lax.axis_index("slide")
+    gy = lax.axis_index("gy")
+    gx = lax.axis_index("gx")
+    zlo, y = gy // 4, gy % 4
+    zhi, core = gx // 2, gx % 2
+    return x, y, zhi * 2 + zlo, core
+
+
+def device_at(x, y, z, core):
+    return (x, (z % 2) * 4 + y, (z // 2) * 2 + core)
+
+
+def neighbour(axis, by):
+    x, y, z, core = coords()
+    if axis == "x":
+        return device_at((x + by + 4) % 4, y, z, core)
+    if axis == "y":
+        return device_at(x, (y + by + 4) % 4, z, core)
+    return device_at(x, y, (z + by + 4) % 4, core)
+
+
+def mate_id():
+    x, y, z, core = coords()
+    return device_at(x, y, z, 1 - core)
+
+
+def axis_coord(axis):
+    x, y, z, _ = coords()
+    return {"x": x, "y": y, "z": z}[axis]
+
+
+def pick(ref, left, axis, j):
+    dims = [d for d in ("x", "l", "y", "h") if (d in left) or (d in "lh" and "z" in left)]
+    index = []
+    for d in dims:
+        if d == axis:
+            index.append(j)
+        elif axis == "z" and d == "l":
+            index.append(j % 2)
+        elif axis == "z" and d == "h":
+            index.append(j // 2)
+        else:
+            index.append(slice(None))
+    return tuple(index)
+
+
+def row_dims(left):
+    out = []
+    if "x" in left:
+        out.append(4)
+    if "z" in left:
+        out.append(2)
+    if "y" in left:
+        out.append(4)
+    if "z" in left:
+        out.append(2)
+    return tuple(out)
+
+
+def remote(src, dst, ssem, rsem, dev):
+    return pltpu.make_async_remote_copy(
+        src_ref=src, dst_ref=dst, send_sem=ssem, recv_sem=rsem,
+        device_id=dev, device_id_type=pl.DeviceIdType.MESH,
+    )
+
+
+def scatter_kernel(inv_root, normed, attended, gproj, branch, out, *scratch):
+    (at_own, at_mate, b_own, b_mate, last_send, last_recv, mate_ss, mate_rs, ring_ss, ring_rs) = scratch[:10]
+    bufs = scratch[10:]
+    sbuf = [[bufs[c * 3 + p] for p in range(3)] for c in range(3)]
+    rbuf = [[bufs[9 + c * 3 + p] for p in range(3)] for c in range(3)]
+    keep = [[bufs[18 + c * 3 + p] for p in range(3)] for c in range(3)]
+    acc = [[bufs[27 + c * 4 + p] for p in range(4)] for c in range(3)]
+    core = coords()[3]
+
+    barrier = pltpu.get_barrier_semaphore()
+    partners = [mate_id()] + [neighbour(a, s) for a in "xyz" for s in (1, -1)]
+    for dev in partners:
+        pl.semaphore_signal(barrier, inc=1, device_id=dev, device_id_type=pl.DeviceIdType.MESH)
+    pl.semaphore_wait(barrier, len(partners))
+
+    mate_copies = []
+    for j in range(4):
+        src = gproj if j < 3 else branch
+        base = j * 1024 if j < 3 else 0
+        cols = pl.ds(pl.multiple_of(base + (1 - core) * 512, 512), 512)
+        mate_copies.append(remote(src.at[:, cols], b_mate.at[j], mate_ss.at[j], mate_rs.at[j], mate_id()))
+        mate_copies[-1].start()
+    for kind, src in enumerate((normed, attended)):
+        at_own[kind] = src[...].T.reshape(at_own.shape[1:])
+        mate_copies.append(
+            remote(at_own.at[kind], at_mate.at[kind], mate_ss.at[4 + kind], mate_rs.at[4 + kind], mate_id())
+        )
+        mate_copies[-1].start()
+    for j in range(4):
+        src = gproj if j < 3 else branch
+        base = j * 1024 if j < 3 else 0
+        cols = pl.ds(pl.multiple_of(base + core * 512, 512), 512)
+        b_own[:, j * 512 : (j + 1) * 512] = src[:, cols]
+    for copy in mate_copies:
+        copy.wait_recv()
+
+    def first_block(c, j):
+        start, count = COLOR_COLS[c]
+        axis = COLOR_AXES[c][0]
+        kind = 1 if c == 2 else 0
+        index = pick(None, "xyz", axis, j)
+        left_own = at_own[(kind,) + index].reshape(256, 256)
+        left_mate = at_mate[(kind,) + index].reshape(256, 256)
+        total = jnp.dot(left_own, b_own[:, start : start + count], preferred_element_type=jnp.float32)
+        parts = []
+        for chunk in range(4):
+            lo, hi = max(start, chunk * 512), min(start + count, (chunk + 1) * 512)
+            if lo < hi:
+                parts.append(
+                    jnp.dot(
+                        left_mate,
+                        b_mate[chunk, :, lo - chunk * 512 : hi - chunk * 512],
+                        preferred_element_type=jnp.float32,
+                    )
+                )
+        return total + jnp.concatenate(parts, axis=1)
+
+    for p in range(3):
+        copies = [[None] * 6 for _ in range(3)]
+
+        def send(c, s):
+            axis = COLOR_AXES[c][p]
+            by = 1 if s in (0, 2, 4) else -1
+            copies[c][s] = remote(
+                sbuf[c][p].at[s], rbuf[c][p].at[s],
+                ring_ss.at[c, p, s], ring_rs.at[c, p, s], neighbour(axis, by),
+            )
+            copies[c][s].start()
+
+        def block(c, by):
+            axis = COLOR_AXES[c][p]
+            j = (axis_coord(axis) + by + 4) % 4
+            if p == 0:
+                return first_block(c, j)
+            ref = acc[c][p - 1]
+            rows = 256 >> (2 * p)
+            return ref[pick(None, COLOR_AXES[c][p:], axis, j)].reshape(rows, COLOR_COLS[c][1])
+
+        for c in range(3):
+            half = COLOR_COLS[c][1] // 2
+            value = block(c, 2)
+            sbuf[c][p][0] = value[:, :half].astype(jnp.bfloat16)
+            send(c, 0)
+            sbuf[c][p][1] = value[:, half:].astype(jnp.bfloat16)
+            send(c, 1)
+        for c in range(3):
+            half = COLOR_COLS[c][1] // 2
+            value = block(c, 1)
+            sbuf[c][p][2] = value[:, half:].astype(jnp.bfloat16)
+            send(c, 2)
+            keep[c][p][0] = value[:, :half]
+            value = block(c, -1)
+            sbuf[c][p][3] = value[:, :half].astype(jnp.bfloat16)
+            send(c, 3)
+            keep[c][p][1] = value[:, half:]
+        own = []
+        for c in range(3):
+            rows = 256 >> (2 * p)
+            shape = acc[c][p].shape
+            acc[c][p][...] = block(c, 0).reshape(shape)
+        for c in range(3):
+            for s in (0, 1):
+                copies[c][s].wait_recv()
+                sbuf[c][p][4 + s] = (keep[c][p][s] + rbuf[c][p][s].astype(jnp.float32)).astype(jnp.bfloat16)
+                send(c, 4 + s)
+        for c in range(3):
+            half = COLOR_COLS[c][1] // 2
+            for s in (2, 3, 4, 5):
+                copies[c][s].wait_recv()
+            shape = acc[c][p].shape
+            lead = shape[:-1]
+            first = rbuf[c][p][3].astype(jnp.float32) + rbuf[c][p][4].astype(jnp.float32)
+            second = rbuf[c][p][2].astype(jnp.float32) + rbuf[c][p][5].astype(jnp.float32)
+            acc[c][p][..., :half] += first.reshape(lead + (half,))
+            acc[c][p][..., half:] += second.reshape(lead + (half,))
+        for c in range(3):
+            for s in range(6):
+                copies[c][s].wait_send()
+
+    for c in range(3):
+        start, count = COLOR_COLS[c]
+        value = acc[c][2][...] * inv_root
+        mine = jnp.where(core == 0, value[:8], value[8:])
+        theirs = jnp.where(core == 0, value[8:], value[:8])
+        last_send[:, start : start + count] = theirs
+        for chunk in range(4):
+            lo, hi = max(start, chunk * 512), min(start + count, (chunk + 1) * 512)
+            if lo < hi:
+                offset = pl.multiple_of(chunk * 1024 + lo - chunk * 512 + core * 512, 256)
+                out[:, pl.ds(offset, hi - lo)] = mine[:, lo - start : hi - start]
+    final = remote(last_send, last_recv, mate_ss.at[6], mate_rs.at[6], mate_id())
+    final.start()
+    final.wait_recv()
+    for chunk in range(4):
+        offset = pl.multiple_of(chunk * 1024 + (1 - core) * 512, 512)
+        out[:, pl.ds(offset, 512)] = last_recv[:, chunk * 512 : (chunk + 1) * 512]
+    final.wait_send()
+    for copy in mate_copies:
+        copy.wait_send()
+
+
+def scatter_weight_grads(normed, attended, gproj, branch, inv_root):
+    bf16, f32 = jnp.bfloat16, jnp.float32
+    scratch = [
+        pltpu.VMEM((2, 4, 2, 4, 2, 16, 256), bf16),
+        pltpu.VMEM((2, 4, 2, 4, 2, 16, 256), bf16),
+        pltpu.VMEM((256, 2048), bf16),
+        pltpu.VMEM((4, 256, 512), bf16),
+        pltpu.VMEM((8, 2048), f32),
+        pltpu.VMEM((8, 2048), f32),
+        pltpu.SemaphoreType.DMA((7,)),
+        pltpu.SemaphoreType.DMA((7,)),
+        pltpu.SemaphoreType.DMA((3, 3, 6)),
+        pltpu.SemaphoreType.DMA((3, 3, 6)),
+    ]
+    for _ in range(2):
+        for c in range(3):
+            for p in range(3):
+                scratch.append(pltpu.VMEM((6, 256 >> (2 * p), COLOR_COLS[c][1] // 2), bf16))
+    for c in range(3):
+        for p in range(3):
+            scratch.append(pltpu.VMEM((2, 256 >> (2 * p), COLOR_COLS[c][1] // 2), f32))
+    for c in range(3):
+        for p in range(4):
+            left = COLOR_AXES[c][p + 1 :]
+            scratch.append(pltpu.VMEM(row_dims(left) + (16, COLOR_COLS[c][1]), f32))
+    return pl.pallas_call(
+        functools.partial(scatter_kernel, inv_root),
+        out_shape=jax.ShapeDtypeStruct((8, 4096), f32),
+        in_specs=[pl.BlockSpec(memory_space=pltpu.VMEM)] * 4,
+        out_specs=pl.BlockSpec(memory_space=pltpu.VMEM),
+        scratch_shapes=scratch,
+        compiler_params=pltpu.CompilerParams(
+            collective_id=0, has_side_effects=True, vmem_limit_bytes=60 << 20
+        ),
+    )(normed, attended, gproj, branch)
 
 
 def local(tokens, weights, norm_gain, tissue, cotangent):
@@ -241,29 +493,8 @@
     input_grad = (upstream + inverse * (scaled - first_mean - normalized * second_mean)).astype(
         jnp.bfloat16
     )
-    weight_grads = lax.psum_scatter(
-        jnp.concatenate(
-            [
-                lax.dot_general(
-                    normed_flat,
-                    grad_projected,
-                    (((0,), (0,)), ((), ())),
-                    preferred_element_type=jnp.float32,
-                )
-                * inv_root,
-                lax.dot_general(
-                    attended_flat,
-                    branch_flat,
-                    (((0,), (0,)), ((), ())),
-                    preferred_element_type=jnp.float32,
-                )
-                * inv_root,
-            ],
-            axis=1,
-        ),
-        ("slide", "gy", "gx"),
-        scatter_dimension=0,
-        tiled=True,
+    weight_grads = scatter_weight_grads(
+        normed_flat, attended_flat, grad_projected, branch_flat, inv_root
     )
     return (block_output[None], input_grad[None], weight_grads)
 

time: 1140 us -> 501 us (0.44)
  waiting for transfers between devices: 695 us -> 29.7 us
  Pallas kernels: 0 us -> 48.9 us
  between operations: 14.7 us -> 1.31 us
    reduce_scatter x1 -> x0, waiting for transfers between devices: 665 us -> none  [local(): lax.psum_scatter(jnp.concatenate([lax.dot_general(normed_flat, grad_proje...]
    pallas_call x0 -> x1, Pallas kernels: none -> 48.9 us  [scatter_weight_grads(): pl.pallas_call(functools.partial(scatter_kernel, inv_root), out_shape=jax...]
  transfers between devices with their start and end apart: 9 -> 8, of which waited for: 8 -> 6; matrix products, arithmetic and copies ran while one was open for 2% -> 4% of each run, Pallas kernels for 0% -> 0%
where the time goes in v1:
time: 501 us; the launch traced here: 492 us
  local copies, waits for them, and re-layouts  180 us (36%)
  matrix products  114 us (23%)
  other arithmetic  59.8 us (12%)
  Pallas kernels  48.9 us (10%)
  waiting for transfers between devices  29.7 us (6%)
  loops' own time  29.4 us (6%)
  starting transfers between devices  29 us (6%)
    dot_general x12, matrix products, contract(): jnp.einsum(pattern, left_operand, second, preferred_element_type=jnp.floa...  99 us
    pallas_call x1, Pallas kernels, scatter_weight_grads(): pl.pallas_call(functools.partial(scatter_kernel, inv_root), out_shape=jax...  48.9 us
    another operation x1, loops' own time, run_strips(): return lax.fori_loop(0, tile_rows // 8, strip_step, start_carry)  29.4 us
    while x50, local copies, waits for them, and re-layouts  25.9 us
    concatenate x4, local copies, waits for them, and re-layouts, tile_attention(): jnp.concatenate([grad_keys.reshape(block_count, window_size, model_width)...  25.9 us
    transpose x4, local copies, waits for them, and re-layouts, contract(): jnp.einsum(pattern, left_operand, second, preferred_element_type=jnp.floa...  25.6 us
    slice x4, local copies, waits for them, and re-layouts, tile_attention(): windows[:, :, :model_width]  19.2 us
    concatenate x2, other arithmetic, tile_attention(): jnp.concatenate([grad_keys.reshape(block_count, window_size, model_width)...  17.9 us
  transfers between devices with their start and end apart: 8, of which 6 were waited for; matrix products, arithmetic and copies ran while one was open for 4% of the time, Pallas kernels for 0%

profile of v1, /device:TPU:1, one launch (start us, length us, event | category | flops | bytes accessed | tf_op | source)
XLA Modules:
  0.0 492.1 jit_solution(8379687321944257573)
XLA Ops:
  4.7 2.3 fusion.102
  7.0 4.8 fusion.75
  13.7 4.7 collective-permute-start
  19.0 8.4 %collective-permute-done.1 = bf16[6,16,2048]{2,0,1:T(8,128)(2,1)S(1)} collective-permute-done((bf16[6,16,2048]{2,0,1:T(8,128)(2,1)S(1)}, bf16[6,16,2048]{2,0,1:T(8,128)(2,1)S(1)}, u32[]{:S(2)}, u32[]{:S(2)}) %collective-permute-start.1) | collective-permute-done | bytes 393248 | tf_op jit(solution)/shard_map/ppermute | solution.py:26
  30.4 7.4 %collective-permute-start.2 = (bf16[28,6,2048]{2,0,1:T(8,128)(2,1)}, bf16[28,6,2048]{2,0,1:T(8,128)(2,1)}, u32[]{:S(2)}, u32[]{:S(2)}) collective-permute-start(bf16[28,6,2048]{2,0,1:T(8,128)(2,1)} %get-tuple-element.607), channel_id=1, source_target_pairs={{0,1},{1,2},{2,3},{4,5},{5,6},{6,7},{8,9},{9,10},{10,11},{12,13},{... | collective-permute-start | bytes 2064392 | tf_op jit(solution)/shard_map/ppermute | solution.py:23
  37.8 1.9 collective-permute-start.3
  39.8 2.5 fusion.95
  42.3 4.7 collective-permute-done.2
  47.0 5.9 %collective-permute-done.3 = bf16[28,6,2048]{2,0,1:T(8,128)(2,1)} collective-permute-done((bf16[28,6,2048]{2,0,1:T(8,128)(2,1)}, bf16[28,6,2048]{2,0,1:T(8,128)(2,1)}, u32[]{:S(2)}, u32[]{:S(2)}) %collective-permute-start.3) | collective-permute-done | bytes 688160 | tf_op jit(solution)/shard_map/ppermute | solution.py:26
  52.9 2.4 pad_maximum_fusion.3
  55.3 3.7 copy.100
  60.7 3.9 broadcast_in_dim.81
  64.5 310.2 %while.33 = (s32[]{:T(128)}, bf16[16,16,1024]{2,1,0:T(8,128)(2,1)}, bf16[16,16,1024]{2,1,0:T(8,128)(2,1)}, f32[28,28,2048]{2,1,0:T(8,128)}, bf16[28,28,2048]{2,1...) while((s32[]{:T(128)}, bf16[16,16,1024]{2,1,0:T(8,128)(2,1)}, ...), condition=%wide.region_8.9_spmd, body=%wide.region_2.8_spmd.sunk | while | flops 662583808 | bytes 314590624 | solution.py:172
  93.9 2.1 constant_dynamic-slice_fusion.6
  98.2 3.4 copy.160
  101.6 3.5 fusion.183
  105.2 4.6 copy.161
  109.8 6.0 %copy.162 = bf16[2,400,1024]{1,2,0:T(8,128)(2,1)} copy(bf16[2,400,1024]{2,0,1:T(2,128)(2,1)} %get-tuple-element.704) | data formatting | bytes 3276800 | tf_op jit(solution)/shard_map/while/body/eval_jaxpr/slice | solution.py:98
  115.8 2.7 fusion.189
  119.2 3.6 fusion.187
  122.8 18.6 %fusion.190 = bf16[2,64,16,64]{1,3,2,0:T(8,128)(2,1)} fusion(bf16[2,400,16,64]{1,3,2,0:T(8,128)(2,1)} %bitcast.338, f32[2,16,64,400]{3,2,1,0:T(8,128)} %fusion.189, f32[2,16,64,400]{3,2,1,0:T(8,128)} %get-tuple-element.711, f32[2,16,64]{2,1,0:T(8,128)S(1)} %get-tuple-element.712), kind=kOutput, calls=%fused_computation.36.clone.1 | convolution fusion | flops 110725520 | bytes 8462336 | tf_op jit(solution)/shard_map/while/body/eval_jaxpr/nhqk,nkhd->nqhd/dot_general | solution.py:38
  141.4 3.8 fusion.188
  145.1 18.6 %fusion.191 = f32[2,400,16,64]{1,3,2,0:T(8,128)} fusion(f32[2,16,64,400]{3,2,1,0:T(8,128)} %fusion.189, bf16[1,2,8,8,16,64]{5,4,3,1,2,0:T(8,128)(2,1)S(1)} %bitcast.343, f32[2,16,64,400]{3,2,1,0:T(8,128)} %get-tuple-element.711, f32[2,16,64]{2,1,0:T(8,128)S(1)} %get-tuple-element.712), kind=kOutput, calls=%fused_computation.20.clone.1 | convolution fusion | flops 110594448 | bytes 10100736 | tf_op jit(solution)/shard_map/while/body/eval_jaxpr/nhqk,nqhd->nkhd/dot_general | solution.py:38
  163.8 5.1 %convolution_bitcast_fusion.2 = f32[2,400,16,64]{1,3,2,0:T(8,128)} fusion(bf16[1,2,8,8,16,64]{5,4,3,1,2,0:T(8,128)(2,1)S(1)} %bitcast.341, f32[2,16,64,400]{3,2,1,0:T(8,128)} %get-tuple-element.711, f32[2,16,64]{2,1,0:T(8,128)S(1)} %get-tuple-element.712), kind=kOutput, calls=%fused_computation.21.clone.1 | convolution fusion | flops 106496000 | bytes 6823936 | tf_op jit(solution)/shard_map/while/body/eval_jaxpr/nhqk,nqhd->nkhd/dot_general | solution.py:38
  172.0 6.4 %copy.166 = f32[2,400,16,64]{3,2,0,1:T(8,128)} copy(f32[2,400,16,64]{1,3,2,0:T(8,128)} %convolution_bitcast_fusion.2) | data formatting | bytes 6553600 | tf_op jit(solution)/shard_map/while/body/eval_jaxpr/nhqk,nqhd->nkhd/transpose | solution.py:38
  178.4 5.8 %concatenate.120 = f32[1,2,20,20,1024]{4,1,3,2,0:T(2,128)S(1)} reshape(f32[2,400,16,64]{3,2,0,1:T(8,128)} %copy.166) | data formatting | bytes 6553600 | tf_op jit(solution)/shard_map/while/body/eval_jaxpr/concatenate | solution.py:114
  184.3 6.4 %copy.167 = f32[2,400,16,64]{3,2,0,1:T(8,128)} copy(f32[2,400,16,64]{1,3,2,0:T(8,128)} %fusion.191) | data formatting | bytes 6553600 | tf_op jit(solution)/shard_map/while/body/eval_jaxpr/nhqk,nqhd->nkhd/transpose | solution.py:38
  190.7 7.1 %concatenate.121 = f32[1,2,20,20,1024]{4,1,3,2,0:T(2,128)} reshape(f32[2,400,16,64]{3,2,0,1:T(8,128)} %copy.167) | data formatting | bytes 6553600 | tf_op jit(solution)/shard_map/while/body/eval_jaxpr/concatenate | solution.py:114
  197.8 9.0 %pad_maximum_fusion.14 = f32[1,2,20,20,2048]{4,1,3,2,0:T(2,128)} fusion(f32[1,2,20,20,1024]{4,1,3,2,0:T(2,128)S(1)} %concatenate.120, f32[1,2,20,20,1024]{4,1,3,2,0:T(2,128)} %concatenate.121), kind=kLoop, calls=%fused_computation.2.clone.1 | loop fusion | flops 1638400 | bytes 13107200 | tf_op jit(solution)/shard_map/while/body/eval_jaxpr/concatenate | solution.py:114
  206.8 6.7 %copy.168 = f32[1,2,20,20,2048]{4,3,2,1,0:T(8,128)S(1)} copy(f32[1,2,20,20,2048]{4,1,3,2,0:T(2,128)} %pad_maximum_fusion.14) | data formatting | bytes 13107200 | tf_op jit(solution)/shard_map/while
  217.5 2.1 fusion.194
  225.5 2.9 copy-done
  234.7 2.1 constant_dynamic-slice_fusion.6
  239.0 3.4 copy.160
  242.4 3.5 fusion.183
  245.9 4.6 copy.161
  250.6 6.0 %copy.162 = bf16[2,400,1024]{1,2,0:T(8,128)(2,1)} copy(bf16[2,400,1024]{2,0,1:T(2,128)(2,1)} %get-tuple-element.704) | data formatting | bytes 3276800 | tf_op jit(solution)/shard_map/while/body/eval_jaxpr/slice | solution.py:98
  256.6 2.7 fusion.189
  260.0 3.6 fusion.187
  263.6 18.6 %fusion.190 = bf16[2,64,16,64]{1,3,2,0:T(8,128)(2,1)} fusion(bf16[2,400,16,64]{1,3,2,0:T(8,128)(2,1)} %bitcast.338, f32[2,16,64,400]{3,2,1,0:T(8,128)} %fusion.189, f32[2,16,64,400]{3,2,1,0:T(8,128)} %get-tuple-element.711, f32[2,16,64]{2,1,0:T(8,128)S(1)} %get-tuple-element.712), kind=kOutput, calls=%fused_computation.36.clone.1 | convolution fusion | flops 110725520 | bytes 8462336 | tf_op jit(solution)/shard_map/while/body/eval_jaxpr/nhqk,nkhd->nqhd/dot_general | solution.py:38
  282.2 3.8 fusion.188
  285.9 18.6 %fusion.191 = f32[2,400,16,64]{1,3,2,0:T(8,128)} fusion(f32[2,16,64,400]{3,2,1,0:T(8,128)} %fusion.189, bf16[1,2,8,8,16,64]{5,4,3,1,2,0:T(8,128)(2,1)S(1)} %bitcast.343, f32[2,16,64,400]{3,2,1,0:T(8,128)} %get-tuple-element.711, f32[2,16,64]{2,1,0:T(8,128)S(1)} %get-tuple-element.712), kind=kOutput, calls=%fused_computation.20.clone.1 | convolution fusion | flops 110594448 | bytes 10100736 | tf_op jit(solution)/shard_map/while/body/eval_jaxpr/nhqk,nqhd->nkhd/dot_general | solution.py:38
  304.6 5.1 %convolution_bitcast_fusion.2 = f32[2,400,16,64]{1,3,2,0:T(8,128)} fusion(bf16[1,2,8,8,16,64]{5,4,3,1,2,0:T(8,128)(2,1)S(1)} %bitcast.341, f32[2,16,64,400]{3,2,1,0:T(8,128)} %get-tuple-element.711, f32[2,16,64]{2,1,0:T(8,128)S(1)} %get-tuple-element.712), kind=kOutput, calls=%fused_computation.21.clone.1 | convolution fusion | flops 106496000 | bytes 6823936 | tf_op jit(solution)/shard_map/while/body/eval_jaxpr/nhqk,nqhd->nkhd/dot_general | solution.py:38
  312.8 6.4 %copy.166 = f32[2,400,16,64]{3,2,0,1:T(8,128)} copy(f32[2,400,16,64]{1,3,2,0:T(8,128)} %convolution_bitcast_fusion.2) | data formatting | bytes 6553600 | tf_op jit(solution)/shard_map/while/body/eval_jaxpr/nhqk,nqhd->nkhd/transpose | solution.py:38
  319.2 5.8 %concatenate.120 = f32[1,2,20,20,1024]{4,1,3,2,0:T(2,128)S(1)} reshape(f32[2,400,16,64]{3,2,0,1:T(8,128)} %copy.166) | data formatting | bytes 6553600 | tf_op jit(solution)/shard_map/while/body/eval_jaxpr/concatenate | solution.py:114
  325.1 6.4 %copy.167 = f32[2,400,16,64]{3,2,0,1:T(8,128)} copy(f32[2,400,16,64]{1,3,2,0:T(8,128)} %fusion.191) | data formatting | bytes 6553600 | tf_op jit(solution)/shard_map/while/body/eval_jaxpr/nhqk,nqhd->nkhd/transpose | solution.py:38
  331.5 7.1 %concatenate.121 = f32[1,2,20,20,1024]{4,1,3,2,0:T(2,128)} reshape(f32[2,400,16,64]{3,2,0,1:T(8,128)} %copy.167) | data formatting | bytes 6553600 | tf_op jit(solution)/shard_map/while/body/eval_jaxpr/concatenate | solution.py:114
  338.6 9.0 %pad_maximum_fusion.14 = f32[1,2,20,20,2048]{4,1,3,2,0:T(2,128)} fusion(f32[1,2,20,20,1024]{4,1,3,2,0:T(2,128)S(1)} %concatenate.120, f32[1,2,20,20,1024]{4,1,3,2,0:T(2,128)} %concatenate.121), kind=kLoop, calls=%fused_computation.2.clone.1 | loop fusion | flops 1638400 | bytes 13107200 | tf_op jit(solution)/shard_map/while/body/eval_jaxpr/concatenate | solution.py:114
  347.6 6.7 %copy.168 = f32[1,2,20,20,2048]{4,3,2,1,0:T(8,128)S(1)} copy(f32[1,2,20,20,2048]{4,1,3,2,0:T(2,128)} %pad_maximum_fusion.14) | data formatting | bytes 13107200 | tf_op jit(solution)/shard_map/while
  358.2 2.1 fusion.194
  366.3 2.9 copy-done
  374.8 6.7 %copy.139 = bf16[28,28,2048]{2,0,1:T(8,128)(2,1)S(1)} copy(f32[28,28,2048]{2,1,0:T(8,128)} %get-tuple-element.553) | data formatting | bytes 9633792 | tf_op jit(solution)/shard_map/while | solution.py:172
  383.5 5.1 %collective-permute-start.5 = (bf16[28,6,2048]{2,0,1:T(8,128)(2,1)S(1)}, bf16[28,6,2048]{2,0,1:T(8,128)(2,1)S(1)}, u32[]{:S(2)}, u32[]{:S(2)}) collective-permute-start(bf16[28,6,2048]{2,0,1:T(8,128)(2,1)S(1)} %get-tuple-element.605), channel_id=1, source_target_pairs={{0,1},{1,2},{2,3},{4,5},{5,6},{6,7},{8,9},{9,10},{10,11},{12,13},{... | collective-permute-start | bytes 2064392 | tf_op jit(solution)/shard_map/ppermute | solution.py:34
  388.7 2.6 slice.1180
  391.3 5.1 %collective-permute-done.4 = bf16[28,6,2048]{2,0,1:T(8,128)(2,1)S(1)} collective-permute-done((bf16[28,6,2048]{2,0,1:T(8,128)(2,1)S(1)}, bf16[28,6,2048]{2,0,1:T(8,128)(2,1)S(1)}, u32[]{:S(2)}, u32[]{:S(2)}) %collective-permute-start.4) | collective-permute-done | bytes 688160 | tf_op jit(solution)/shard_map/ppermute | solution.py:34
  396.9 8.5 %scatter-add.44 = f32[28,16,2048]{2,1,0:T(8,128)} dynamic-update-slice(f32[28,16,2048]{2,1,0:T(8,128)} %slice.1180, f32[28,6,2048]{2,1,0:T(8,128)S(1)} %convert_add_fusion, s32[]{:T(128)} %constant.779.clone.1, s32[]{:T(128)} %constant.791.clone.1, s32[]{:T(128)} %constant.779.clone.1) | dynamic-update-slice | bytes 2752516 | tf_op jit(solution)/shard_map/scatter-add | solution.py:474
  405.4 2.0 slice_add_fusion.1
  407.4 9.3 %scatter-add.54 = f32[28,16,2048]{2,1,0:T(8,128)} dynamic-update-slice(f32[28,16,2048]{2,1,0:T(8,128)} %scatter-add.44, f32[28,6,2048]{2,1,0:T(8,128)S(1)} %slice_add_fusion.1, s32[]{:T(128)} %constant.779.clone.1, s32[]{:T(128)} %constant.779.clone.1, s32[]{:T(128)} %constant.779.clone.1) | dynamic-update-slice | bytes 2752516 | tf_op jit(solution)/shard_map/scatter-add | solution.py:476
  416.7 2.4 convert.12
  420.8 3.1 fusion.98
  424.1 5.1 %collective-permute-start.7 = (bf16[6,16,2048]{2,1,0:T(8,128)(2,1)S(1)}, bf16[6,16,2048]{2,1,0:T(8,128)(2,1)S(1)}, u32[]{:S(2)}, u32[]{:S(2)}) collective-permute-start(bf16[6,16,2048]{2,1,0:T(8,128)(2,1)S(1)} %get-tuple-element.609), channel_id=1, source_target_pairs={{0,4},{4,8},{8,12},{12,16},{16,20},{20,24},{24,28},{1,5},{5,9},{9,... | collective-permute-start | bytes 1179656 | tf_op jit(solution)/shard_map/ppermute | solution.py:34
  429.3 4.4 collective-permute-done.7
  434.1 4.7 fusion.117
  440.1 48.9 %shard_map.76 = f32[8,4096]{1,0:T(8,128)} custom-call(bf16[256,1024]{1,0:T(8,128)(2,1)} %copy-done.11, bf16[256,1024]{1,0:T(8,128)(2,1)S(1)} %bitcast.349, bf16[256,3072]{1,0:T(8,128)(2,1)} %bitcast.344, bf16[256,1024]{1,0:T(8,128)(2,1)} %get-tuple-element.618.branch), custom_call_target="tpu_custom_call" | custom-call | tf_op jit(solution)/shard_map/pallas_call | solution.py:412
  (232 shorter events, 63.9 us)
Async XLA Ops:
  1.8 10.0 %copy-start.17 = (f32[16,16]{1,0:T(8,128)}, f32[16,16]{1,0:T(8,128)S(1)}, u32[]{:S(2)}) copy-start(f32[16,16]{1,0:T(8,128)S(1)} %broadcast_multiply_fusion.2) | copy-start | bytes 3076
  3.2 8.6 %copy-start.19 = (f32[16,16]{1,0:T(8,128)}, f32[16,16]{1,0:T(8,128)S(1)}, u32[]{:S(2)}) copy-start(f32[16,16]{1,0:T(8,128)S(1)} %add_rsqrt_fusion) | copy-start | bytes 3076
  7.0 4.8 copy-start.11
  12.2 15.3 %collective-permute-start.1 = (bf16[6,16,2048]{2,0,1:T(8,128)(2,1)S(1)}, bf16[6,16,2048]{2,0,1:T(8,128)(2,1)S(1)}, u32[]{:S(2)}, u32[]{:S(2)}) collective-permute-start(bf16[6,16,2048]{2,0,1:T(8,128)(2,1)S(1)} %copy.117), channel_id=1, source_target_pairs={{4,0},{8,4},{12,8},{16,12},{20,16},{24,20},{28,24},{5,1},{9,5},{13... | collective-permute-start | bytes 1179656 | tf_op jit(solution)/shard_map/ppermute | solution.py:26
  13.7 14.9 %collective-permute-start = (bf16[6,16,2048]{2,0,1:T(8,128)(2,1)S(1)}, bf16[6,16,2048]{2,0,1:T(8,128)(2,1)S(1)}, u32[]{:S(2)}, u32[]{:S(2)}) collective-permute-start(bf16[6,16,2048]{2,0,1:T(8,128)(2,1)S(1)} %copy.115), channel_id=1, source_target_pairs={{0,4},{4,8},{8,12},{12,16},{16,20},{20,24},{24,28},{1,5},{5,9},{9,... | collective-permute-start | bytes 1179656 | tf_op jit(solution)/shard_map/ppermute | solution.py:23
  30.4 16.6 %collective-permute-start.2 = (bf16[28,6,2048]{2,0,1:T(8,128)(2,1)}, bf16[28,6,2048]{2,0,1:T(8,128)(2,1)}, u32[]{:S(2)}, u32[]{:S(2)}) collective-permute-start(bf16[28,6,2048]{2,0,1:T(8,128)(2,1)} %get-tuple-element.607), channel_id=1, source_target_pairs={{0,1},{1,2},{2,3},{4,5},{5,6},{6,7},{8,9},{9,10},{10,11},{12,13},{... | collective-permute-start | bytes 2064392 | tf_op jit(solution)/shard_map/ppermute | solution.py:23
  37.8 15.1 %collective-permute-start.3 = (bf16[28,6,2048]{2,0,1:T(8,128)(2,1)}, bf16[28,6,2048]{2,0,1:T(8,128)(2,1)}, u32[]{:S(2)}, u32[]{:S(2)}) collective-permute-start(bf16[28,6,2048]{2,0,1:T(8,128)(2,1)} %get-tuple-element.608), channel_id=1, source_target_pairs={{1,0},{2,1},{3,2},{5,4},{6,5},{7,6},{9,8},{10,9},{11,10},{13,12},{... | collective-permute-start | bytes 2064392 | tf_op jit(solution)/shard_map/ppermute | solution.py:26
  58.9 5.6 %copy-start.21 = (s32[5]{0:T(128)S(1)}, s32[5]{0:T(128)}, u32[]{:S(2)}) copy-start(s32[5]{0:T(128)} %constant.775.clone.1) | copy-start | bytes 64
  87.7 8.7 %copy-start.7 = (bf16[16,16,1024]{2,1,0:T(8,128)(2,1)}, bf16[16,16,1024]{2,1,0:T(8,128)(2,1)S(1)}, u32[]{:S(2)}) copy-start(bf16[16,16,1024]{2,1,0:T(8,128)(2,1)S(1)} %get-tuple-element.760) | copy-start | bytes 1572868 | tf_op jit(solution)/shard_map/while
  87.7 8.7 %copy-start.9 = (bf16[16,16,1024]{2,1,0:T(8,128)(2,1)}, bf16[16,16,1024]{2,1,0:T(8,128)(2,1)S(1)}, u32[]{:S(2)}) copy-start(bf16[16,16,1024]{2,1,0:T(8,128)(2,1)S(1)} %get-tuple-element.761) | copy-start | bytes 1572868 | tf_op jit(solution)/shard_map/while
  115.8 2.7 copy-start.2
  163.8 5.2 %copy-start.5 = (bf16[2,64,16,64]{1,3,2,0:T(8,128)(2,1)S(1)}, bf16[2,64,16,64]{1,3,2,0:T(8,128)(2,1)}, u32[]{:S(2)}) copy-start(bf16[2,64,16,64]{1,3,2,0:T(8,128)(2,1)} %fusion.188) | copy-start | bytes 786436 | tf_op jit(solution)/shard_map/while
  163.8 5.9 %copy-start.4 = (bf16[2,64,16,64]{1,3,2,0:T(8,128)(2,1)S(1)}, bf16[2,64,16,64]{1,3,2,0:T(8,128)(2,1)}, u32[]{:S(2)}) copy-start(bf16[2,64,16,64]{1,3,2,0:T(8,128)(2,1)} %fusion.190) | copy-start | bytes 786436 | tf_op jit(solution)/shard_map/while
  163.8 6.7 %copy-start.12 = (bf16[16,16,1024]{2,1,0:T(8,128)(2,1)S(1)}, bf16[16,16,1024]{2,1,0:T(8,128)(2,1)}, u32[]{:S(2)}) copy-start(bf16[16,16,1024]{2,1,0:T(8,128)(2,1)} %get-tuple-element.737) | copy-start | bytes 1572868 | tf_op jit(solution)/shard_map/while
  171.3 0.8 copy-start.13
  220.9 1.9 slice-start
  221.2 2.9 slice-start.1
  224.1 4.4 copy-start.8
  224.1 4.4 copy-start.10
  225.5 2.9 copy-start
  228.5 8.7 %copy-start.7 = (bf16[16,16,1024]{2,1,0:T(8,128)(2,1)}, bf16[16,16,1024]{2,1,0:T(8,128)(2,1)S(1)}, u32[]{:S(2)}) copy-start(bf16[16,16,1024]{2,1,0:T(8,128)(2,1)S(1)} %get-tuple-element.760) | copy-start | bytes 1572868 | tf_op jit(solution)/shard_map/while
  228.5 8.7 %copy-start.9 = (bf16[16,16,1024]{2,1,0:T(8,128)(2,1)}, bf16[16,16,1024]{2,1,0:T(8,128)(2,1)S(1)}, u32[]{:S(2)}) copy-start(bf16[16,16,1024]{2,1,0:T(8,128)(2,1)S(1)} %get-tuple-element.761) | copy-start | bytes 1572868 | tf_op jit(solution)/shard_map/while
  256.6 2.7 copy-start.2
  304.5 5.2 %copy-start.5 = (bf16[2,64,16,64]{1,3,2,0:T(8,128)(2,1)S(1)}, bf16[2,64,16,64]{1,3,2,0:T(8,128)(2,1)}, u32[]{:S(2)}) copy-start(bf16[2,64,16,64]{1,3,2,0:T(8,128)(2,1)} %fusion.188) | copy-start | bytes 786436 | tf_op jit(solution)/shard_map/while
  304.5 5.9 %copy-start.4 = (bf16[2,64,16,64]{1,3,2,0:T(8,128)(2,1)S(1)}, bf16[2,64,16,64]{1,3,2,0:T(8,128)(2,1)}, u32[]{:S(2)}) copy-start(bf16[2,64,16,64]{1,3,2,0:T(8,128)(2,1)} %fusion.190) | copy-start | bytes 786436 | tf_op jit(solution)/shard_map/while
  304.6 6.7 %copy-start.12 = (bf16[16,16,1024]{2,1,0:T(8,128)(2,1)S(1)}, bf16[16,16,1024]{2,1,0:T(8,128)(2,1)}, u32[]{:S(2)}) copy-start(bf16[16,16,1024]{2,1,0:T(8,128)(2,1)} %get-tuple-element.737) | copy-start | bytes 1572868 | tf_op jit(solution)/shard_map/while
  312.0 0.8 copy-start.13
  361.7 1.9 slice-start
  362.0 2.9 slice-start.1
  364.9 4.4 copy-start.8
  364.9 4.4 copy-start.10
  366.3 2.9 copy-start
  374.7 13.9 %copy-start.1 = (f32[28,28,2048]{2,1,0:T(8,128)S(1)}, f32[28,28,2048]{2,1,0:T(8,128)}, u32[]{:S(2)}) copy-start(f32[28,28,2048]{2,1,0:T(8,128)} %get-tuple-element.553) | copy-start | bytes 19267588
  381.6 14.8 %collective-permute-start.4 = (bf16[28,6,2048]{2,0,1:T(8,128)(2,1)S(1)}, bf16[28,6,2048]{2,0,1:T(8,128)(2,1)S(1)}, u32[]{:S(2)}, u32[]{:S(2)}) collective-permute-start(bf16[28,6,2048]{2,0,1:T(8,128)(2,1)S(1)} %get-tuple-element.606), channel_id=1, source_target_pairs={{1,0},{2,1},{3,2},{5,4},{6,5},{7,6},{9,8},{10,9},{11,10},{13,12},{... | collective-permute-start | bytes 2064392 | tf_op jit(solution)/shard_map/ppermute | solution.py:34
  383.5 21.9 %collective-permute-start.5 = (bf16[28,6,2048]{2,0,1:T(8,128)(2,1)S(1)}, bf16[28,6,2048]{2,0,1:T(8,128)(2,1)S(1)}, u32[]{:S(2)}, u32[]{:S(2)}) collective-permute-start(bf16[28,6,2048]{2,0,1:T(8,128)(2,1)S(1)} %get-tuple-element.605), channel_id=1, source_target_pairs={{0,1},{1,2},{2,3},{4,5},{5,6},{6,7},{8,9},{9,10},{10,11},{12,13},{... | collective-permute-start | bytes 2064392 | tf_op jit(solution)/shard_map/ppermute | solution.py:34
  416.7 4.0 copy-start.6
  416.7 4.0 copy-start.14
  416.7 4.0 copy-start.22
  419.1 4.8 copy-start.3
  419.2 10.1 %collective-permute-start.6 = (bf16[6,16,2048]{2,1,0:T(8,128)(2,1)S(1)}, bf16[6,16,2048]{2,1,0:T(8,128)(2,1)S(1)}, u32[]{:S(2)}, u32[]{:S(2)}) collective-permute-start(bf16[6,16,2048]{2,1,0:T(8,128)(2,1)S(1)} %get-tuple-element.610), channel_id=1, source_target_pairs={{4,0},{8,4},{12,8},{16,12},{20,16},{24,20},{28,24},{5,1},{9,5},{13... | collective-permute-start | bytes 1179656 | tf_op jit(solution)/shard_map/ppermute | solution.py:34
  424.1 10.0 %copy-start.16 = (bf16[16,16,1024]{2,1,0:T(8,128)(2,1)S(1)}, bf16[16,16,1024]{2,1,0:T(8,128)(2,1)}, u32[]{:S(2)}) copy-start(bf16[16,16,1024]{2,1,0:T(8,128)(2,1)} %get-tuple-element.552) | copy-start | bytes 1572868
  424.1 10.0 %copy-start.18 = (f32[16,16]{1,0:T(8,128)S(1)}, f32[16,16]{1,0:T(8,128)}, u32[]{:S(2)}) copy-start(f32[16,16]{1,0:T(8,128)} %copy-done.17) | copy-start | bytes 3076
  424.1 10.0 %copy-start.20 = (f32[16,16]{1,0:T(8,128)S(1)}, f32[16,16]{1,0:T(8,128)}, u32[]{:S(2)}) copy-start(f32[16,16]{1,0:T(8,128)} %copy-done.19) | copy-start | bytes 3076
  424.1 10.0 %copy-start.23 = (f32[1024]{0:T(1024)S(1)}, f32[1024]{0:T(1024)}, u32[]{:S(2)}) copy-start(f32[1024]{0:T(1024)} %param.35) | copy-start | bytes 12292
  424.1 9.6 %collective-permute-start.7 = (bf16[6,16,2048]{2,1,0:T(8,128)(2,1)S(1)}, bf16[6,16,2048]{2,1,0:T(8,128)(2,1)S(1)}, u32[]{:S(2)}, u32[]{:S(2)}) collective-permute-start(bf16[6,16,2048]{2,1,0:T(8,128)(2,1)S(1)} %get-tuple-element.609), channel_id=1, source_target_pairs={{0,4},{4,8},{8,12},{12,16},{16,20},{20,24},{24,28},{1,5},{5,9},{9,... | collective-permute-start | bytes 1179656 | tf_op jit(solution)/shard_map/ppermute | solution.py:34
  438.8 50.2 %copy-start.15 = (bf16[1,16,16,1024]{3,2,1,0:T(8,128)(2,1)S(1)}, bf16[1,16,16,1024]{3,2,1,0:T(8,128)(2,1)}, u32[]{:S(2)}) copy-start(bf16[1,16,16,1024]{3,2,1,0:T(8,128)(2,1)} %param.37) | copy-start | bytes 1572868

commit v2 on v1

v2 whole, which is shorter than its diff:
```python
import functools
import math

import jax
import jax.numpy as jnp
from jax import lax
from jax.experimental import pallas as pl
from jax.experimental.pallas import tpu as pltpu
from jax.sharding import PartitionSpec as P

EPSILON = 1e-06


COLOR_COLS = ((0, 768), (768, 768), (1536, 512))
COLOR_AXES = ("xyz", "yzx", "zxy")


def coords():
    x = lax.axis_index("slide")
    gy = lax.axis_index("gy")
    gx = lax.axis_index("gx")
    zlo, y = gy // 4, gy % 4
    zhi, core = gx // 2, gx % 2
    return x, y, zhi * 2 + zlo, core


def device_at(x, y, z, core):
    return (x, (z % 2) * 4 + y, (z // 2) * 2 + core)


def neighbour(axis, by):
    x, y, z, core = coords()
    if axis == "x":
        return device_at((x + by + 4) % 4, y, z, core)
    if axis == "y":
        return device_at(x, (y + by + 4) % 4, z, core)
    return device_at(x, y, (z + by + 4) % 4, core)


def mate_id():
    x, y, z, core = coords()
    return device_at(x, y, z, 1 - core)


def axis_coord(axis):
    x, y, z, _ = coords()
    return {"x": x, "y": y, "z": z}[axis]


def pick(ref, left, axis, j):
    dims = [d for d in ("x", "l", "y", "h") if (d in left) or (d in "lh" and "z" in left)]
    index = []
    for d in dims:
        if d == axis:
            index.append(j)
        elif axis == "z" and d == "l":
            index.append(j % 2)
        elif axis == "z" and d == "h":
            index.append(j // 2)
        else:
            index.append(slice(None))
    return tuple(index)


def row_dims(left):
    out = []
    if "x" in left:
        out.append(4)
    if "z" in left:
        out.append(2)
    if "y" in left:
        out.append(4)
    if "z" in left:
        out.append(2)
    return tuple(out)


def remote(src, dst, ssem, rsem, dev):
    return pltpu.make_async_remote_copy(
        src_ref=src, dst_ref=dst, send_sem=ssem, recv_sem=rsem,
        device_id=dev, device_id_type=pl.DeviceIdType.MESH,
    )


def scatter_kernel(inv_root, normed, attended, gproj, branch, out, *scratch):
    (at_own, at_mate, b_own, b_mate, last_send, last_recv, mate_ss, mate_rs, ring_ss, ring_rs) = scratch[:10]
    bufs = scratch[10:]
    sbuf = [[bufs[c * 3 + p] for p in range(3)] for c in range(3)]
    rbuf = [[bufs[9 + c * 3 + p] for p in range(3)] for c in range(3)]
    keep = [[bufs[18 + c * 3 + p] for p in range(3)] for c in range(3)]
    acc = [[bufs[27 + c * 4 + p] for p in range(4)] for c in range(3)]
    core = coords()[3]

    barrier = pltpu.get_barrier_semaphore()
    partners = [mate_id()] + [neighbour(a, s) for a in "xyz" for s in (1, -1)]
    for dev in partners:
        pl.semaphore_signal(barrier, inc=1, device_id=dev, device_id_type=pl.DeviceIdType.MESH)
    pl.semaphore_wait(barrier, len(partners))

    mate_copies = []
    for j in range(4):
        src = gproj if j < 3 else branch
        base = j * 1024 if j < 3 else 0
        cols = pl.ds(pl.multiple_of(base + (1 - core) * 512, 512), 512)
        mate_copies.append(remote(src.at[:, cols], b_mate.at[j], mate_ss.at[j], mate_rs.at[j], mate_id()))
        mate_copies[-1].start()
    for kind, src in enumerate((normed, attended)):
        at_own[kind] = src[...].T.reshape(at_own.shape[1:])
        mate_copies.append(
            remote(at_own.at[kind], at_mate.at[kind], mate_ss.at[4 + kind], mate_rs.at[4 + kind], mate_id())
        )
        mate_copies[-1].start()
    for j in range(4):
        src = gproj if j < 3 else branch
        base = j * 1024 if j < 3 else 0
        cols = pl.ds(pl.multiple_of(base + core * 512, 512), 512)
        b_own[:, j * 512 : (j + 1) * 512] = src[:, cols]
    for copy in mate_copies:
        copy.wait_recv()

    def first_block(c, j):
        start, count = COLOR_COLS[c]
        axis = COLOR_AXES[c][0]
        kind = 1 if c == 2 else 0
        index = pick(None, "xyz", axis, j)
        left_own = at_own[(kind,) + index].reshape(256, 256)
        left_mate = at_mate[(kind,) + index].reshape(256, 256)
        total = jnp.dot(left_own, b_own[:, start : start + count], preferred_element_type=jnp.float32)
        parts = []
        for chunk in range(4):
            lo, hi = max(start, chunk * 512), min(start + count, (chunk + 1) * 512)
            if lo < hi:
                parts.append(
                    jnp.dot(
                        left_mate,
                        b_mate[chunk, :, lo - chunk * 512 : hi - chunk * 512],
                        preferred_element_type=jnp.float32,
                    )
                )
        return total + jnp.concatenate(parts, axis=1)

    for p in range(3):
        copies = [[None] * 6 for _ in range(3)]

        def send(c, s):
            axis = COLOR_AXES[c][p]
            by = 1 if s in (0, 2, 4) else -1
            copies[c][s] = remote(
                sbuf[c][p].at[s], rbuf[c][p].at[s],
                ring_ss.at[c, p, s], ring_rs.at[c, p, s], neighbour(axis, by),
            )
            copies[c][s].start()

        def block(c, by):
            axis = COLOR_AXES[c][p]
            j = (axis_coord(axis) + by + 4) % 4
            if p == 0:
                return first_block(c, j)
            ref = acc[c][p - 1]
            rows = 256 >> (2 * p)
            return ref[pick(None, COLOR_AXES[c][p:], axis, j)].reshape(rows, COLOR_COLS[c][1])

        for c in range(3):
            half = COLOR_COLS[c][1] // 2
            value = block(c, 2)
            sbuf[c][p][0] = value[:, :half].astype(jnp.bfloat16)
            send(c, 0)
            sbuf[c][p][1] = value[:, half:].astype(jnp.bfloat16)
            send(c, 1)
        for c in range(3):
            half = COLOR_COLS[c][1] // 2
            value = block(c, 1)
            sbuf[c][p][2] = value[:, half:].astype(jnp.bfloat16)
            send(c, 2)
            keep[c][p][0] = value[:, :half]
            value = block(c, -1)
            sbuf[c][p][3] = value[:, :half].astype(jnp.bfloat16)
            send(c, 3)
            keep[c][p][1] = value[:, half:]
        own = []
        for c in range(3):
            rows = 256 >> (2 * p)
            shape = acc[c][p].shape
            acc[c][p][...] = block(c, 0).reshape(shape)
        for c in range(3):
            for s in (0, 1):
                copies[c][s].wait_recv()
                sbuf[c][p][4 + s] = (keep[c][p][s] + rbuf[c][p][s].astype(jnp.float32)).astype(jnp.bfloat16)
                send(c, 4 + s)
        for c in range(3):
            half = COLOR_COLS[c][1] // 2
            for s in (2, 3, 4, 5):
                copies[c][s].wait_recv()
            shape = acc[c][p].shape
            lead = shape[:-1]
            first = rbuf[c][p][3].astype(jnp.float32) + rbuf[c][p][4].astype(jnp.float32)
            second = rbuf[c][p][2].astype(jnp.float32) + rbuf[c][p][5].astype(jnp.float32)
            acc[c][p][..., :half] += first.reshape(lead + (half,))
            acc[c][p][..., half:] += second.reshape(lead + (half,))
        for c in range(3):
            for s in range(6):
                copies[c][s].wait_send()

    for c in range(3):
        start, count = COLOR_COLS[c]
        value = acc[c][2][...] * inv_root
        mine = jnp.where(core == 0, value[:8], value[8:])
        theirs = jnp.where(core == 0, value[8:], value[:8])
        last_send[:, start : start + count] = theirs
        for chunk in range(4):
            lo, hi = max(start, chunk * 512), min(start + count, (chunk + 1) * 512)
            if lo < hi:
                offset = pl.multiple_of(chunk * 1024 + lo - chunk * 512 + core * 512, 256)
                out[:, pl.ds(offset, hi - lo)] = mine[:, lo - start : hi - start]
    final = remote(last_send, last_recv, mate_ss.at[6], mate_rs.at[6], mate_id())
    final.start()
    final.wait_recv()
    for chunk in range(4):
        offset = pl.multiple_of(chunk * 1024 + (1 - core) * 512, 512)
        out[:, pl.ds(offset, 512)] = last_recv[:, chunk * 512 : (chunk + 1) * 512]
    final.wait_send()
    for copy in mate_copies:
        copy.wait_send()


def scatter_weight_grads(normed, attended, gproj, branch, inv_root):
    bf16, f32 = jnp.bfloat16, jnp.float32
    scratch = [
        pltpu.VMEM((2, 4, 2, 4, 2, 16, 256), bf16),
        pltpu.VMEM((2, 4, 2, 4, 2, 16, 256), bf16),
        pltpu.VMEM((256, 2048), bf16),
        pltpu.VMEM((4, 256, 512), bf16),
        pltpu.VMEM((8, 2048), f32),
        pltpu.VMEM((8, 2048), f32),
        pltpu.SemaphoreType.DMA((7,)),
        pltpu.SemaphoreType.DMA((7,)),
        pltpu.SemaphoreType.DMA((3, 3, 6)),
        pltpu.SemaphoreType.DMA((3, 3, 6)),
    ]
    for _ in range(2):
        for c in range(3):
            for p in range(3):
                scratch.append(pltpu.VMEM((6, 256 >> (2 * p), COLOR_COLS[c][1] // 2), bf16))
    for c in range(3):
        for p in range(3):
            scratch.append(pltpu.VMEM((2, 256 >> (2 * p), COLOR_COLS[c][1] // 2), f32))
    for c in range(3):
        for p in range(4):
            left = COLOR_AXES[c][p + 1 :]
            scratch.append(pltpu.VMEM(row_dims(left) + (16, COLOR_COLS[c][1]), f32))
    return pl.pallas_call(
        functools.partial(scatter_kernel, inv_root),
        out_shape=jax.ShapeDtypeStruct((8, 4096), f32),
        in_specs=[pl.BlockSpec(memory_space=pltpu.VMEM)] * 4,
        out_specs=pl.BlockSpec(memory_space=pltpu.VMEM),
        scratch_shapes=scratch,
        compiler_params=pltpu.CompilerParams(
            collective_id=0, has_side_effects=True, vmem_limit_bytes=60 << 20
        ),
    )(normed, attended, gproj, branch)


def dot_nn(left, right):
    return jnp.dot(left, right, preferred_element_type=jnp.float32)


def dot_nt(left, right):
    return lax.dot_general(left, right, (((1,), (1,)), ((), ())), preferred_element_type=jnp.float32)


def dot_tn(left, right):
    return lax.dot_general(left, right, (((0,), (0,)), ((), ())), preferred_element_type=jnp.float32)


def head_diagonal(full):
    low = lax.broadcasted_iota(jnp.int32, (64, 128), 1) < 64
    first = jnp.where(low, full[0:64, 0:128], full[64:128, 0:128])
    second = jnp.where(low, full[128:192, 128:256], full[192:256, 128:256])
    return jnp.concatenate([first, second], axis=1)


def attention_kernel(
    projected, projected_rows, grad_attn, attended, gproj,
    pad, queries, upstream, bias, acc,
    side_send, side_recv, back_send, back_recv, rows_send, rows_recv,
    load_sem, rows_ss, rows_rs, side_ss, side_rs, back_ss, back_rs, up_ss, up_rs,
):
    f32, bf16 = jnp.float32, jnp.bfloat16
    slide = lax.axis_index("slide")
    gy = lax.axis_index("gy")
    gx = lax.axis_index("gx")
    beside = ((slide, gy, gx - 1), (slide, gy, gx + 1))
    along = ((slide, gy - 1, gx), (slide, gy + 1, gx))
    has_beside = (gx > 0, gx < 3)
    has_along = (gy > 0, gy < 7)

    loads = []
    for g in range(4):
        for kv in range(2):
            lo = 1024 * (kv + 1) + 256 * g
            loads.append(
                pltpu.make_async_copy(
                    projected.at[:, :, lo : lo + 256], pad.at[g, kv, 6:22, 0:16, :], load_sem.at[2 * g + kv]
                )
            )
            loads[-1].start()
    query_load = pltpu.make_async_copy(projected_rows.at[:, :, 0:1024], queries, load_sem.at[8])
    query_load.start()
    upstream_load = pltpu.make_async_copy(grad_attn, upstream, load_sem.at[9])
    upstream_load.start()

    barrier = pltpu.get_barrier_semaphore()
    greeted = (
        (slide, gy, (gx + 3) % 4), (slide, gy, (gx + 1) % 4),
        (slide, (gy + 7) % 8, gx), (slide, (gy + 1) % 8, gx),
    )
    for dev in greeted:
        pl.semaphore_signal(barrier, inc=1, device_id=dev, device_id_type=pl.DeviceIdType.MESH)
    pl.semaphore_wait(barrier, 4)

    def rows_copy(g, side):
        src = (6, 16)[side]
        dst = (22, 0)[side]
        return remote(
            pad.at[g, :, src : src + 6, 0:16, :], pad.at[g, :, dst : dst + 6, 0:16, :],
            rows_ss.at[g, side], rows_rs.at[g, side], along[side],
        )

    def side_copy(g, side):
        return remote(
            side_send.at[g, side], side_recv.at[g, side], side_ss.at[g, side], side_rs.at[g, side], beside[side]
        )

    def back_copy(g, side):
        return remote(
            back_send.at[g, side], back_recv.at[g, side], back_ss.at[g, side], back_rs.at[g, side], beside[side]
        )

    def up_copy(g, side):
        return remote(
            rows_send.at[g, side], rows_recv.at[g, side], up_ss.at[g, side], up_rs.at[g, side], along[side]
        )

    for g in range(4):
        for kv in range(2):
            loads[2 * g + kv].wait()
        for side in range(2):
            @pl.when(has_along[side])
            def _(g=g, side=side):
                rows_copy(g, side).start()

    for b in range(4):
        shape = (512, 128)
        key = lax.broadcasted_iota(jnp.int32, shape, 0)
        lane = lax.broadcasted_iota(jnp.int32, shape, 1) & 63
        key_row, slot = key >> 5, key & 31
        key_col = jnp.where(slot < 24, slot, slot - 32)
        down = key_row - (lane >> 4)
        across = key_col - (lane & 15)
        grid_row = key_row + (gy * 16 + 4 * b - 6)
        grid_col = key_col + gx * 16
        allowed = (down >= 0) & (down <= 12) & (across >= -6) & (across <= 6)
        allowed = allowed & (grid_row >= 0) & (grid_row < 128) & (grid_col >= 0) & (grid_col < 64)
        half = jnp.where(allowed, 0.0, -1e30).astype(f32)
        bias[b] = jnp.concatenate([half, half], axis=1)

    query_load.wait()
    upstream_load.wait()

    for g in range(4):
        for side in range(2):
            zero_row = (22, 0)[side]

            @pl.when(has_along[side])
            def _(g=g, side=side):
                rows_copy(g, 1 - side).wait_recv()

            @pl.when(jnp.logical_not(has_along[side]))
            def _(g=g, zero_row=(0, 22)[side]):
                pad[g, :, zero_row : zero_row + 6, 0:16, :] = jnp.zeros((2, 6, 16, 256), bf16)

        inner = pad[g, :, :, 0:16, :].astype(f32)
        side_send[g, 0] = inner[:, :, 0:8, :].astype(bf16)
        side_send[g, 1] = inner[:, :, 8:16, :].astype(bf16)
        for side in range(2):
            @pl.when(has_beside[side])
            def _(g=g, side=side):
                side_copy(g, side).start()

    same_head = (lax.broadcasted_iota(jnp.int32, (256, 256), 0) >> 6) == (
        lax.broadcasted_iota(jnp.int32, (256, 256), 1) >> 6
    )
    head_mask = jnp.where(same_head, 1.0, 0.0).astype(bf16)

    def attend(g):
        columns = slice(256 * g, 256 * g + 256)
        acc[g] = jnp.zeros((2, 28, 32, 256), f32)

        def block(b, carry):
            keys = pad[g, 0, pl.ds(4 * b, 16)].reshape(512, 256)
            values = pad[g, 1, pl.ds(4 * b, 16)].reshape(512, 256)
            query = queries[b, :, columns] * jnp.asarray(0.125, bf16)
            grad = upstream[b, :, columns]
            query_heads = jnp.concatenate([query] * 4, axis=0) * head_mask
            grad_heads = jnp.concatenate([grad] * 4, axis=0) * head_mask
            scores = dot_nt(keys, query_heads) + bias[b]
            top = jnp.max(scores, axis=0, keepdims=True)
            exponent = jnp.exp(scores - top)
            total = jnp.sum(exponent, axis=0, keepdims=True)
            probs = exponent * (1.0 / total)
            probs_bf = probs.astype(bf16)
            grad_probs = dot_nt(values, grad_heads)
            centre = jnp.sum(probs * grad_probs, axis=0, keepdims=True)
            grad_scores = (probs * (grad_probs - centre)).astype(bf16)
            attended[b, :, columns] = head_diagonal(dot_tn(probs_bf, values)).astype(bf16)
            gproj[b, :, columns] = (head_diagonal(dot_tn(grad_scores, keys)) * 0.125).astype(bf16)
            rows = pl.ds(4 * b, 16)
            acc[g, 0, rows] += dot_nn(grad_scores, query_heads).reshape(16, 32, 256)
            acc[g, 1, rows] += dot_nn(probs_bf, grad_heads).reshape(16, 32, 256)
            return carry

        lax.fori_loop(0, 4, block, 0)

    def start_back(g):
        back_send[g, 0] = acc[g, :, :, 24:32, :].astype(bf16)
        back_send[g, 1] = acc[g, :, :, 16:24, :].astype(bf16)
        for side in range(2):
            @pl.when(has_beside[side])
            def _(side=side):
                back_copy(g, side).start()

    def start_up(g):
        for side in range(2):
            lo = (0, 8)[side]

            @pl.when(has_beside[side])
            def _(side=side, lo=lo):
                back_copy(g, 1 - side).wait_recv()
                acc[g, :, :, lo : lo + 8, :] += back_recv[g, 1 - side].astype(f32)

        rows_send[g, 0] = acc[g, :, 0:6, 0:16, :].astype(bf16)
        rows_send[g, 1] = acc[g, :, 22:28, 0:16, :].astype(bf16)
        for side in range(2):
            @pl.when(has_along[side])
            def _(side=side):
                up_copy(g, side).start()

    def finish(g):
        for side in range(2):
            lo = (6, 16)[side]

            @pl.when(has_along[side])
            def _(side=side, lo=lo):
                up_copy(g, 1 - side).wait_recv()
                acc[g, :, lo : lo + 6, 0:16, :] += rows_recv[g, 1 - side].astype(f32)

        for kv in range(2):
            lo = 1024 * (kv + 1) + 256 * g
            gproj[:, :, lo : lo + 256] = acc[g, kv, 6:22, 0:16, :].reshape(4, 64, 256).astype(bf16)

    for g in range(4):
        for side in range(2):
            @pl.when(has_beside[side])
            def _(g=g, side=side):
                side_copy(g, 1 - side).wait_recv()

            @pl.when(jnp.logical_not(has_beside[side]))
            def _(g=g, side=side):
                side_recv[g, 1 - side] = jnp.zeros((2, 28, 8, 256), bf16)

        outer = jnp.concatenate([side_recv[g, 0].astype(f32), side_recv[g, 1].astype(f32)], axis=2)
        pad[g, :, :, 16:32, :] = outer.astype(bf16)
        attend(g)
        start_back(g)
        if g >= 1:
            start_up(g - 1)
        if g >= 2:
            finish(g - 2)
    start_up(3)
    finish(2)
    finish(3)
    for g in range(4):
        for side in range(2):
            @pl.when(has_along[side])
            def _(g=g, side=side):
                rows_copy(g, side).wait_send()
                up_copy(g, side).wait_send()

            @pl.when(has_beside[side])
            def _(g=g, side=side):
                side_copy(g, side).wait_send()
                back_copy(g, side).wait_send()


def attention(projected, grad_attn):
    bf16, f32 = jnp.bfloat16, jnp.float32
    dma = pltpu.SemaphoreType.DMA
    any_space = pl.BlockSpec(memory_space=pl.ANY)
    vmem = pl.BlockSpec(memory_space=pltpu.VMEM)
    attended, gproj = pl.pallas_call(
        attention_kernel,
        out_shape=(
            jax.ShapeDtypeStruct((4, 64, 1024), bf16),
            jax.ShapeDtypeStruct((4, 64, 3072), bf16),
        ),
        in_specs=[any_space] * 3,
        out_specs=(vmem, vmem),
        scratch_shapes=[
            pltpu.VMEM((4, 2, 28, 32, 256), bf16),
            pltpu.VMEM((4, 64, 1024), bf16),
            pltpu.VMEM((4, 64, 1024), bf16),
            pltpu.VMEM((4, 512, 256), f32),
            pltpu.VMEM((4, 2, 28, 32, 256), f32),
            pltpu.VMEM((4, 2, 2, 28, 8, 256), bf16),
            pltpu.VMEM((4, 2, 2, 28, 8, 256), bf16),
            pltpu.VMEM((4, 2, 2, 28, 8, 256), bf16),
            pltpu.VMEM((4, 2, 2, 28, 8, 256), bf16),
            pltpu.VMEM((4, 2, 2, 6, 16, 256), bf16),
            pltpu.VMEM((4, 2, 2, 6, 16, 256), bf16),
            dma((10,)),
        ] + [dma((4, 2))] * 8,
        compiler_params=pltpu.CompilerParams(
            collective_id=1, has_side_effects=True, vmem_limit_bytes=62 << 20
        ),
    )(
        projected.reshape(16, 16, 3072),
        projected.reshape(4, 64, 3072),
        grad_attn.reshape(4, 64, 1024),
    )
    return attended.reshape(256, 1024), gproj.reshape(256, 3072)


def local(tokens, weights, norm_gain, tissue, cotangent):
    model_width = tokens.shape[-1]
    token_count = tokens.shape[1] * tokens.shape[2]
    group_count = lax.axis_size("slide") * lax.axis_size("gy") * lax.axis_size("gx")
    inv_root = 1.0 / math.sqrt(group_count * token_count)
    weight_in = weights[:, : 3 * model_width]
    weight_out = weights[:, 3 * model_width :]
    tokens_float = tokens.reshape(token_count, model_width).astype(jnp.float32)
    row_mean = jnp.mean(tokens_float, axis=-1, keepdims=True)
    centered = tokens_float - row_mean
    variance = jnp.mean(centered * centered, axis=-1, keepdims=True)
    inverse = lax.rsqrt(variance + EPSILON)
    normalized = centered * inverse
    normed = (normalized * norm_gain).astype(jnp.bfloat16)
    projected = jnp.dot(normed, weight_in, preferred_element_type=jnp.float32).astype(jnp.bfloat16)
    tissue_mask = tissue.reshape(token_count, 1).astype(jnp.float32)
    upstream = cotangent.reshape(token_count, model_width).astype(jnp.float32)
    branch_grad = (tissue_mask * upstream).astype(jnp.bfloat16)
    grad_attn = jnp.dot(branch_grad, weight_out.T, preferred_element_type=jnp.float32).astype(
        jnp.bfloat16
    )
    attended, grad_projected = attention(projected, grad_attn)
    projection = jnp.dot(attended, weight_out, preferred_element_type=jnp.float32)
    block_output = (tokens_float + tissue_mask * projection).astype(jnp.bfloat16)
    grad_normed = jnp.dot(grad_projected, weight_in.T, preferred_element_type=jnp.float32)
    scaled = grad_normed * norm_gain
    first_mean = jnp.mean(scaled, axis=-1, keepdims=True)
    second_mean = jnp.mean(scaled * normalized, axis=-1, keepdims=True)
    input_grad = (upstream + inverse * (scaled - first_mean - normalized * second_mean)).astype(
        jnp.bfloat16
    )
    weight_grads = scatter_weight_grads(normed, attended, grad_projected, branch_grad, inv_root)
    return (block_output.reshape(tokens.shape), input_grad.reshape(tokens.shape), weight_grads)


def solution(mesh):
    in_specs = (
        P("slide", "gy", "gx", None),
        P(),
        P(),
        P("slide", "gy", "gx"),
        P("slide", "gy", "gx", None),
    )
    out_specs = (
        P("slide", "gy", "gx", None),
        P("slide", "gy", "gx", None),
        P(("slide", "gy", "gx"), None),
    )
    return jax.shard_map(local, mesh=mesh, in_specs=in_specs, out_specs=out_specs, check_vma=False)
```

time: 501 us -> 122 us (0.24); the launches traced: 492 us -> 122 us
  local copies, waits for them, and re-layouts: 180 us -> 0.93 us
  matrix products: 114 us -> 17.6 us
  other arithmetic: 59.8 us -> 7.19 us
  Pallas kernels: 48.9 us -> 95.2 us
  waiting for transfers between devices: 29.7 us -> 0 us
  loops' own time: 29.4 us -> 0 us
  starting transfers between devices: 29 us -> 0 us
    dot_general x15 -> x3, matrix products: 109 us -> 12.2 us  [the longest x1 5.72 us: local(): jnp.dot(normed, weight_in, preferred_element_type=jnp.float32)]
    pallas_call x0 -> x1, Pallas kernels: none -> 52.3 us  [attention(): pl.pallas_call(attention_kernel, out_shape=(jax.ShapeDtypeStruct((4, 64,...]
    while x52 -> x0, local copies, waits for them, and re-layouts: 36.3 us -> none
    transpose x8 -> x0, local copies, waits for them, and re-layouts: 33 us -> none  [the longest x4 25.6 us: contract(): jnp.einsum(pattern, left_operand, second, preferred_element_type=jnp.floa...]
    slice x15 -> x0, local copies, waits for them, and re-layouts: 31.7 us -> none  [the longest x4 19.2 us: tile_attention(): windows[:, :, :model_width]]
    ppermute x8 -> x0, waiting for transfers between devices: 29.7 us -> none  [the longest x2 14.3 us: with_halo(): lax.ppermute(lax.slice_in_dim(block, 0, width, axis=dim), axis, backward)]
    another operation x1 -> x0, loops' own time: 29.4 us -> none  [run_strips(): return lax.fori_loop(0, tile_rows // 8, strip_step, start_carry)]
    ppermute x8 -> x0, starting transfers between devices: 29 us -> none  [the longest x4 13.7 us: shifted(): return lax.ppermute(shard, axis, pairs)]
  transfers between devices with their start and end apart: 8 -> 0, of which waited for: 6 -> 0; matrix products, arithmetic and copies ran while one was open for 4% -> 0% of each run, Pallas kernels for 0% -> 0%
where the time goes in v2:
time: 122 us
  Pallas kernels  95.2 us (78%)
  matrix products  17.6 us (14%)
  other arithmetic  7.19 us (6%)
    pallas_call x1, Pallas kernels, attention(): pl.pallas_call(attention_kernel, out_shape=(jax.ShapeDtypeStruct((4, 64,...  52.3 us
    pallas_call x1, Pallas kernels, scatter_weight_grads(): pl.pallas_call(functools.partial(scatter_kernel, inv_root), out_shape=jax...  42.8 us
    dot_general x1, matrix products, local(): jnp.dot(normed, weight_in, preferred_element_type=jnp.float32)  5.72 us
    dot_general x1, matrix products, local(): jnp.dot(grad_projected, weight_in.T, preferred_element_type=jnp.float32)  5.36 us
    dot_general x1, matrix products, local(): jnp.dot(branch_grad, weight_out.T, preferred_element_type=jnp.float32)  3.32 us
    dot_general x1, matrix products, local(): jnp.dot(attended, weight_out, preferred_element_type=jnp.float32)  3.15 us

profile of v2, /device:TPU:1, one launch (start us, length us, event | category | flops | bytes accessed | tf_op | source)
XLA Modules:
  0.0 121.6 jit_solution(8428840591336001481)
XLA Ops:
  0.6 0.7 convert_element_type.47
  1.3 0.1 convert_element_type.48
  1.4 1.2 convert_reduce_fusion
  2.6 0.1 div.15
  2.7 1.3 %multiply_reduce_fusion.1 = f32[16,16]{1,0:T(8,128)S(1)} fusion(bf16[1,16,16,1024]{3,2,1,0:T(8,128)(2,1)} %param.5, f32[16,16]{1,0:T(8,128)S(1)} %broadcast_multiply_fusion), kind=kLoop, calls=%fused_computation.22 | loop fusion | flops 1048320 | bytes 526336 | tf_op jit(solution)/shard_map/reduce_sum | solution.py:543
  4.0 0.1 rsqrt.12
  4.1 1.3 %multiply_convert_fusion.normed = bf16[256,1024]{1,0:T(8,128)(2,1)S(1)} fusion(bf16[1,16,16,1024]{3,2,1,0:T(8,128)(2,1)} %param.5, f32[1024]{0:T(1024)} %param.7, f32[256]{0:T(256)S(1)} %rsqrt.12, f32[256]{0:T(256)S(1)} %div.15), kind=kLoop, calls=%fused_computation.21 | loop fusion | flops 1310720 | bytes 1054720 | tf_op jit(solution)/shard_map/convert_element_type | solution.py:546
  5.5 0.0 copy-start.3
  5.5 1.4 %fusion.26.branch = bf16[256,1024]{1,0:T(8,128)(2,1)S(1)} fusion(bf16[1,16,16,1024]{3,2,1,0:T(8,128)(2,1)} %param.9, f32[256]{0:T(256)S(1)} %convert_element_type.48), kind=kLoop, calls=%fused_computation.16 | loop fusion | flops 786432 | bytes 1049600 | tf_op jit(solution)/shard_map/convert_element_type | solution.py:550
  6.9 0.0 copy-start.2
  6.9 3.3 %fusion.23 = bf16[256,1024]{1,0:T(8,128)(2,1)} fusion(bf16[256,1024]{1,0:T(8,128)(2,1)S(1)} %fusion.26.branch, bf16[1024,4096]{1,0:T(8,128)(2,1)} %param.6), kind=kOutput, calls=%fused_computation.15 | convolution fusion | flops 537133056 | bytes 3145728 | tf_op jit(solution)/shard_map/dot_general | solution.py:551
  10.2 5.7 %fusion.4 = bf16[256,3072]{1,0:T(8,128)(2,1)} fusion(bf16[256,1024]{1,0:T(8,128)(2,1)S(1)} %multiply_convert_fusion.normed, bf16[1024,4096]{1,0:T(8,128)(2,1)} %param.6), kind=kOutput, calls=%fused_computation.4 | convolution fusion | flops 1611399168 | bytes 8388608 | tf_op jit(solution)/shard_map/dot_general | solution.py:547
  15.9 0.0 copy-done.3
  15.9 0.0 copy-done.2
  15.9 0.0 copy-start
  15.9 0.0 copy-start.6
  15.9 52.3 %shard_map.76 = (bf16[4,64,1024]{2,1,0:T(8,128)(2,1)}, bf16[4,64,3072]{2,1,0:T(8,128)(2,1)}) custom-call(bf16[16,16,3072]{2,1,0:T(8,128)(2,1)} %bitcast.27, bf16[4,64,3072]{2,1,0:T(8,128)(2,1)} %bitcast.28, bf16[4,64,1024]{2,1,0:T(8,128)(2,1)} %bitcast.34), custom_call_target="tpu_custom_call" | custom-call | tf_op jit(solution)/shard_map/pallas_call | solution.py:500
  68.3 42.8 %shard_map.77 = f32[8,4096]{1,0:T(8,128)} custom-call(bf16[256,1024]{1,0:T(8,128)(2,1)} %copy-done.3, bf16[256,1024]{1,0:T(8,128)(2,1)} %bitcast.32, bf16[256,3072]{1,0:T(8,128)(2,1)} %bitcast.29, bf16[256,1024]{1,0:T(8,128)(2,1)} %copy-done.2), custom_call_target="tpu_custom_call" | custom-call | tf_op jit(solution)/shard_map/pallas_call | solution.py:251
  111.1 0.0 copy-done
  111.1 0.0 copy-done.6
  111.1 0.0 copy-start.4
  111.1 0.0 copy-start.1
  111.1 5.4 %fusion.29 = (f32[256]{0:T(256)S(1)}, f32[256]{0:T(256)S(1)}, f32[256,1024]{1,0:T(8,128)S(1)}) fusion(f32[256]{0:T(256)S(1)} %rsqrt.12, f32[256]{0:T(256)S(1)} %div.15, bf16[1,16,16,1024]{3,2,1,0:T(8,128)(2,1)S(1)} %copy-done, f32[1024]{0:T(1024)S(1)} %copy-done.6, bf16[256,3072]{1,0:T(8,128)(2,1)} %bitcast.30, bf16[1024,4096]{1,0:T(8,128)(2,1)} %param.6), kind=kOutput, calls=%fused_computation.28 | convolution fusion | flops 1612447232 | bytes 9445376 | tf_op jit(solution)/shard_map/dot_general | solution.py:557
  116.5 0.0 copy-done.4
  116.5 0.0 copy-start.5
  116.5 3.2 %fusion.20 = bf16[256,1024]{1,0:T(8,128)(2,1)} fusion(bf16[256,1024]{1,0:T(8,128)(2,1)S(1)} %bitcast.33, bf16[1024,4096]{1,0:T(8,128)(2,1)} %param.6, f32[256]{0:T(256)S(1)} %convert_element_type.48, bf16[256,1024]{1,0:T(8,128)(2,1)S(1)} %bitcast.26), kind=kOutput, calls=%fused_computation.14 | convolution fusion | flops 537919488 | bytes 3671040 | tf_op jit(solution)/shard_map/dot_general | solution.py:555
  119.7 0.0 copy-done.1
  119.7 1.3 %fusion.27 = bf16[256,1024]{1,0:T(8,128)(2,1)} fusion(f32[256,1024]{1,0:T(8,128)S(1)} %get-tuple-element.9, bf16[1,16,16,1024]{3,2,1,0:T(8,128)(2,1)S(1)} %copy-done, bf16[1,16,16,1024]{3,2,1,0:T(8,128)(2,1)S(1)} %copy-done.1, f32[256]{0:T(256)S(1)} %get-tuple-element.10, f32[256]{0:T(256)S(1)} %get-tuple-element.11, f32[256]{0:T(256)S(1)} %rsqrt.12, ...), kind=kLoop, calls=%fused_computation.17 | loop fusion | flops 2621440 | bytes 2625536 | tf_op jit(solution)/shard_map/convert_element_type | solution.py:561
  120.9 0.0 copy-done.5
  120.9 0.7 copy.9
  (3 shorter events, 0.0 us)
Async XLA Ops:
  5.5 10.5 %copy-start.3 = (bf16[256,1024]{1,0:T(8,128)(2,1)}, bf16[256,1024]{1,0:T(8,128)(2,1)S(1)}, u32[]{:S(2)}) copy-start(bf16[256,1024]{1,0:T(8,128)(2,1)S(1)} %multiply_convert_fusion.normed) | copy-start | bytes 1572868
  6.9 9.1 %copy-start.2 = (bf16[256,1024]{1,0:T(8,128)(2,1)}, bf16[256,1024]{1,0:T(8,128)(2,1)S(1)}, u32[]{:S(2)}) copy-start(bf16[256,1024]{1,0:T(8,128)(2,1)S(1)} %fusion.26.branch) | copy-start | bytes 1572868
  15.9 95.2 %copy-start = (bf16[1,16,16,1024]{3,2,1,0:T(8,128)(2,1)S(1)}, bf16[1,16,16,1024]{3,2,1,0:T(8,128)(2,1)}, u32[]{:S(2)}) copy-start(bf16[1,16,16,1024]{3,2,1,0:T(8,128)(2,1)} %param.5) | copy-start | bytes 1572868
  15.9 95.2 %copy-start.6 = (f32[1024]{0:T(1024)S(1)}, f32[1024]{0:T(1024)}, u32[]{:S(2)}) copy-start(f32[1024]{0:T(1024)} %param.7) | copy-start | bytes 12292
  111.1 5.4 %copy-start.4 = (bf16[4,64,1024]{2,1,0:T(8,128)(2,1)S(1)}, bf16[4,64,1024]{2,1,0:T(8,128)(2,1)}, u32[]{:S(2)}) copy-start(bf16[4,64,1024]{2,1,0:T(8,128)(2,1)} %get-tuple-element.5) | copy-start | bytes 1572868
  111.1 8.5 %copy-start.1 = (bf16[1,16,16,1024]{3,2,1,0:T(8,128)(2,1)S(1)}, bf16[1,16,16,1024]{3,2,1,0:T(8,128)(2,1)}, u32[]{:S(2)}) copy-start(bf16[1,16,16,1024]{3,2,1,0:T(8,128)(2,1)} %param.9) | copy-start | bytes 1572868
  116.5 4.4 %copy-start.5 = (f32[8,4096]{1,0:T(8,128)S(1)}, f32[8,4096]{1,0:T(8,128)}, u32[]{:S(2)}) copy-start(f32[8,4096]{1,0:T(8,128)} %shard_map.77) | copy-start | bytes 393220

commit v3 on v2

v3 whole, which is shorter than its diff:
```python
import functools
import math

import jax
import jax.numpy as jnp
from jax import lax
from jax.experimental import pallas as pl
from jax.experimental.pallas import tpu as pltpu
from jax.sharding import PartitionSpec as P

EPSILON = 1e-06


LOADED_UP = 0
LOADED_DOWN = 3
CHUNK_AXES = ("xyz", "yzx", "zxy", "xzy")


def coords():
    x = lax.axis_index("slide")
    gy = lax.axis_index("gy")
    gx = lax.axis_index("gx")
    zlo, y = gy // 4, gy % 4
    zhi, core = gx // 2, gx % 2
    return x, y, zhi * 2 + zlo, core


def device_at(x, y, z, core):
    return (x, (z % 2) * 4 + y, (z // 2) * 2 + core)


def neighbour(axis, by):
    x, y, z, core = coords()
    if axis == "x":
        return device_at((x + by + 4) % 4, y, z, core)
    if axis == "y":
        return device_at(x, (y + by + 4) % 4, z, core)
    return device_at(x, y, (z + by + 4) % 4, core)


def mate_id():
    x, y, z, core = coords()
    return device_at(x, y, z, 1 - core)


def axis_coord(axis):
    x, y, z, _ = coords()
    return {"x": x, "y": y, "z": z}[axis]


def pick(ref, left, axis, j):
    dims = [d for d in ("x", "l", "y", "h") if (d in left) or (d in "lh" and "z" in left)]
    index = []
    for d in dims:
        if d == axis:
            index.append(j)
        elif axis == "z" and d == "l":
            index.append(j % 2)
        elif axis == "z" and d == "h":
            index.append(j // 2)
        else:
            index.append(slice(None))
    return tuple(index)


def row_dims(left):
    out = []
    if "x" in left:
        out.append(4)
    if "z" in left:
        out.append(2)
    if "y" in left:
        out.append(4)
    if "z" in left:
        out.append(2)
    return tuple(out)


def remote(src, dst, ssem, rsem, dev):
    return pltpu.make_async_remote_copy(
        src_ref=src, dst_ref=dst, send_sem=ssem, recv_sem=rsem,
        device_id=dev, device_id_type=pl.DeviceIdType.MESH,
    )


def dot_nn(left, right):
    return jnp.dot(left, right, preferred_element_type=jnp.float32)


def dot_nt(left, right):
    return lax.dot_general(left, right, (((1,), (1,)), ((), ())), preferred_element_type=jnp.float32)


def dot_tn(left, right):
    return lax.dot_general(left, right, (((0,), (0,)), ((), ())), preferred_element_type=jnp.float32)


def head_diagonal(full):
    low = lax.broadcasted_iota(jnp.int32, (64, 128), 1) < 64
    first = jnp.where(low, full[0:64, 0:128], full[64:128, 0:128])
    second = jnp.where(low, full[128:192, 128:256], full[192:256, 128:256])
    return jnp.concatenate([first, second], axis=1)


def pack_columns(slab):
    parts = slab.reshape(7, 4, 8, 128)
    place = lax.broadcasted_iota(jnp.int32, (7, 8, 128), 1)
    one = pltpu.roll(parts[:, 1], 6, 1)
    two = pltpu.roll(parts[:, 2], 4, 1)
    three = pltpu.roll(parts[:, 3], 2, 1)
    return (
        jnp.where(place < 6, parts[:, 0], one),
        jnp.where(place < 4, one, two),
        jnp.where(place < 2, two, three),
    )


def unpack_columns(first, second, third):
    place = lax.broadcasted_iota(jnp.int32, (7, 8, 128), 1)
    rows = (
        first,
        pltpu.roll(jnp.where(place < 4, second, first), 2, 1),
        pltpu.roll(jnp.where(place < 2, third, second), 4, 1),
        pltpu.roll(third, 6, 1),
    )
    return jnp.stack(rows, axis=1).reshape(28, 8, 128)


def sublayer_kernel(
    inv_root,
    projected, projected_rows, grad_attn, weights, normed, branch, tokens, cotangent, tissue, gain,
    block_output, input_grad, weight_grads,
    attended, gproj, weight_vmem, grad_normed,
    pad, queries, upstream, bias, acc,
    side_send, side_recv, back_send, back_recv, rows_send, rows_recv, side_relay, back_relay,
    at_own, at_mate, b_mate, last_send, last_recv,
    load_sem, rows_ss, rows_rs, up_ss, up_rs, side_ss, side_rs, back_ss, back_rs,
    far_ss, far_rs, far_relay_ss, far_relay_rs, farb_ss, farb_rs, farb_relay_ss, farb_relay_rs,
    swap_ss, swap_rs, grad_ss, grad_rs, ring_ss, ring_rs,
    *ring_bufs,
):
    f32, bf16 = jnp.float32, jnp.bfloat16
    slide = lax.axis_index("slide")
    gy = lax.axis_index("gy")
    gx = lax.axis_index("gx")
    _, y, z, core = coords()
    along = ((slide, gy - 1, gx), (slide, gy + 1, gx))
    has_along = (gy > 0, gy < 7)
    outer = (gx == 0) | (gx == 3)
    inner = jnp.logical_not(outer)
    mate = mate_id()
    signs = (1, jnp.where(y == LOADED_UP, -1, 1), jnp.where(y == LOADED_DOWN, 1, -1), -1)

    def opposite(by):
        other = (z + by + 4) % 4
        high = other // 2
        return (slide, (other % 2) * 4 + y, jnp.where(outer, high + 1, 3 * high))

    across = [opposite(sign) for sign in signs]

    loads = []
    for g in range(4):
        for kv in range(2):
            lo = 1024 * (kv + 1) + 256 * g
            loads.append(
                pltpu.make_async_copy(
                    projected.at[:, :, lo : lo + 256], pad.at[g, kv, 6:22, 0:16, :], load_sem.at[2 * g + kv]
                )
            )
            loads[-1].start()
    query_load = pltpu.make_async_copy(projected_rows.at[:, :, 0:1024], queries, load_sem.at[8])
    query_load.start()
    upstream_load = pltpu.make_async_copy(grad_attn, upstream, load_sem.at[9])
    upstream_load.start()
    weight_load = pltpu.make_async_copy(weights, weight_vmem, load_sem.at[10])
    weight_load.start()

    barrier = pltpu.get_barrier_semaphore()
    greeted = [mate, (slide, (gy + 7) % 8, gx), (slide, (gy + 1) % 8, gx), opposite(1), opposite(-1)]
    greeted += [neighbour(axis, by) for axis in "xyz" for by in (1, -1)]
    for dev in greeted:
        pl.semaphore_signal(barrier, inc=1, device_id=dev, device_id_type=pl.DeviceIdType.MESH)
    pl.semaphore_wait(barrier, len(greeted))

    def rows_copy(g, side):
        src = (6, 16)[side]
        dst = (22, 0)[side]
        return remote(
            pad.at[g, :, src : src + 6, 0:16, :], pad.at[g, :, dst : dst + 6, 0:16, :],
            rows_ss.at[g, side], rows_rs.at[g, side], along[side],
        )

    def mate_copy(g, sent, got, ss, rs):
        return remote(sent.at[g, 1 - core], got.at[g, 1 - core], ss.at[g], rs.at[g], mate)

    def far_copy(g, kv, sent, relay, ss, rs):
        return remote(sent.at[g, core, kv], relay.at[g, kv], ss.at[g, kv], rs.at[g, kv], across[kv])

    def relay_copy(g, kv, relay, got, ss, rs):
        source = (z - signs[kv] + 4) % 4
        return remote(
            relay.at[g, kv], got.at[g, 1 - source // 2, kv], ss.at[g, kv], rs.at[g, kv], across[kv]
        )

    def side_start(g):
        mate_copy(g, side_send, side_recv, side_ss, side_rs).start()

        @pl.when(inner)
        def _():
            for kv in range(4):
                far_copy(g, kv, side_send, side_relay, far_ss, far_rs).start()

    def side_forward(g):
        @pl.when(outer)
        def _():
            for kv in range(4):
                far_copy(g, kv, side_send, side_relay, far_ss, far_rs).wait_recv()
                relay_copy(g, kv, side_relay, side_recv, far_relay_ss, far_relay_rs).start()

    def side_wait(g):
        mate_copy(g, side_send, side_recv, side_ss, side_rs).wait_recv()

        @pl.when(inner)
        def _():
            for kv in range(4):
                relay_copy(g, kv, side_relay, side_recv, far_relay_ss, far_relay_rs).wait_recv()

    def back_start(g):
        mate_copy(g, back_send, back_recv, back_ss, back_rs).start()

        @pl.when(inner)
        def _():
            for kv in range(4):
                far_copy(g, kv, back_send, back_relay, farb_ss, farb_rs).start()

    def back_forward(g):
        @pl.when(outer)
        def _():
            for kv in range(4):
                far_copy(g, kv, back_send, back_relay, farb_ss, farb_rs).wait_recv()
                relay_copy(g, kv, back_relay, back_recv, farb_relay_ss, farb_relay_rs).start()

    def back_wait(g):
        mate_copy(g, back_send, back_recv, back_ss, back_rs).wait_recv()

        @pl.when(inner)
        def _():
            for kv in range(4):
                relay_copy(g, kv, back_relay, back_recv, farb_relay_ss, farb_relay_rs).wait_recv()

    def drain(g):
        mate_copy(g, side_send, side_recv, side_ss, side_rs).wait_send()
        mate_copy(g, back_send, back_recv, back_ss, back_rs).wait_send()

        @pl.when(inner)
        def _():
            for kv in range(4):
                far_copy(g, kv, side_send, side_relay, far_ss, far_rs).wait_send()
                far_copy(g, kv, back_send, back_relay, farb_ss, farb_rs).wait_send()

        @pl.when(outer)
        def _():
            for kv in range(4):
                relay_copy(g, kv, side_relay, side_recv, far_relay_ss, far_relay_rs).wait_send()
                relay_copy(g, kv, back_relay, back_recv, farb_relay_ss, farb_relay_rs).wait_send()

        for side in range(2):
            @pl.when(has_along[side])
            def _(side=side):
                rows_copy(g, side).wait_send()
                up_copy(g, side).wait_send()

    def up_copy(g, side):
        return remote(
            rows_send.at[g, side], rows_recv.at[g, side], up_ss.at[g, side], up_rs.at[g, side], along[side]
        )

    for g in range(4):
        for kv in range(2):
            loads[2 * g + kv].wait()
        for side in range(2):
            @pl.when(has_along[side])
            def _(g=g, side=side):
                rows_copy(g, side).start()

    for b in range(4):
        shape = (512, 128)
        key = lax.broadcasted_iota(jnp.int32, shape, 0)
        lane = lax.broadcasted_iota(jnp.int32, shape, 1) & 63
        key_row, slot = key >> 5, key & 31
        key_col = jnp.where(slot < 24, slot, slot - 30)
        down = key_row - (lane >> 4)
        aside = key_col - (lane & 15)
        grid_row = key_row + (gy * 16 + 4 * b - 6)
        grid_col = key_col + gx * 16
        allowed = (slot < 30) & (down >= 0) & (down <= 12) & (aside >= -6) & (aside <= 6)
        allowed = allowed & (grid_row >= 0) & (grid_row < 128) & (grid_col >= 0) & (grid_col < 64)
        half = jnp.where(allowed, 0.0, -1e30).astype(f32)
        bias[b] = jnp.concatenate([half, half], axis=1)

    def prepare(g):
        for side in range(2):
            zero_row = (22, 0)[side]

            @pl.when(has_along[side])
            def _(g=g, side=side):
                rows_copy(g, 1 - side).wait_recv()

            @pl.when(jnp.logical_not(has_along[side]))
            def _(g=g, zero_row=(0, 22)[side]):
                pad[g, :, zero_row : zero_row + 6, 0:16, :] = jnp.zeros((2, 6, 16, 256), bf16)

        tile_part = pad[g, :, :, 0:16, :].astype(f32)
        for piece in range(4):
            lanes = slice(128 * (piece % 2), 128 * (piece % 2) + 128)
            part = tile_part[piece // 2, :, :, lanes]
            for side, slab in ((0, part[:, 0:8]), (1, pltpu.roll(part[:, 8:16], 6, 1))):
                for n, packed in enumerate(pack_columns(slab)):
                    side_send[g, side, piece, :, n] = packed.astype(bf16)
        side_start(g)

    @pl.when(outer)
    def _():
        side_recv[:, pl.ds(1 - core, 1)] = jnp.zeros((4, 1, 4, 7, 3, 8, 128), bf16)
        back_recv[:, pl.ds(1 - core, 1)] = jnp.zeros((4, 1, 4, 7, 3, 8, 128), bf16)

    same_head = (lax.broadcasted_iota(jnp.int32, (256, 256), 0) >> 6) == (
        lax.broadcasted_iota(jnp.int32, (256, 256), 1) >> 6
    )
    head_mask = jnp.where(same_head, 1.0, 0.0).astype(bf16)

    def attend(g):
        columns = slice(256 * g, 256 * g + 256)
        acc[g] = jnp.zeros((2, 28, 32, 256), f32)

        def block(b, carry):
            keys = pad[g, 0, pl.ds(4 * b, 16)].reshape(512, 256)
            values = pad[g, 1, pl.ds(4 * b, 16)].reshape(512, 256)
            query = queries[b, :, columns] * jnp.asarray(0.125, bf16)
            grad = upstream[b, :, columns]
            query_heads = jnp.concatenate([query] * 4, axis=0) * head_mask
            grad_heads = jnp.concatenate([grad] * 4, axis=0) * head_mask
            scores = dot_nt(keys, query_heads) + bias[b]
            top = jnp.max(scores, axis=0, keepdims=True)
            exponent = jnp.exp(scores - top)
            total = jnp.sum(exponent, axis=0, keepdims=True)
            probs = exponent * (1.0 / total)
            probs_bf = probs.astype(bf16)
            grad_probs = dot_nt(values, grad_heads)
            centre = jnp.sum(probs * grad_probs, axis=0, keepdims=True)
            grad_scores = (probs * (grad_probs - centre)).astype(bf16)
            attended[b, :, columns] = head_diagonal(dot_tn(probs_bf, values)).astype(bf16)
            gproj[b, :, columns] = (head_diagonal(dot_tn(grad_scores, keys)) * 0.125).astype(bf16)
            rows = pl.ds(4 * b, 16)
            acc[g, 0, rows] += dot_nn(grad_scores, query_heads).reshape(16, 32, 256)
            acc[g, 1, rows] += dot_nn(probs_bf, grad_heads).reshape(16, 32, 256)
            return carry

        lax.fori_loop(0, 4, block, 0)

    def start_back(g):
        for piece in range(4):
            lanes = slice(128 * (piece % 2), 128 * (piece % 2) + 128)
            for side, lo in ((0, 24), (1, 16)):
                for n, packed in enumerate(pack_columns(acc[g, piece // 2, :, lo : lo + 8, lanes])):
                    back_send[g, side, piece, :, n] = packed.astype(bf16)
        back_start(g)

    def start_up(g):
        back_wait(g)
        place = lax.broadcasted_iota(jnp.int32, (28, 8, 128), 1)
        for piece in range(4):
            lanes = slice(128 * (piece % 2), 128 * (piece % 2) + 128)
            low, high = [
                jnp.where(
                    place < 6,
                    unpack_columns(*[back_recv[g, n, piece, :, m].astype(f32) for m in range(3)]),
                    0.0,
                )
                for n in (1, 0)
            ]
            acc[g, piece // 2, :, 0:8, lanes] += low
            acc[g, piece // 2, :, 8:16, lanes] += pltpu.roll(high, 2, 1)
        rows_send[g, 0] = acc[g, :, 0:6, 0:16, :].astype(bf16)
        rows_send[g, 1] = acc[g, :, 22:28, 0:16, :].astype(bf16)
        for side in range(2):
            @pl.when(has_along[side])
            def _(side=side):
                up_copy(g, side).start()

    def finish(g):
        for side in range(2):
            lo = (6, 16)[side]

            @pl.when(has_along[side])
            def _(side=side, lo=lo):
                up_copy(g, 1 - side).wait_recv()
                acc[g, :, lo : lo + 6, 0:16, :] += rows_recv[g, 1 - side].astype(f32)

        for kv in range(2):
            lo = 1024 * (kv + 1) + 256 * g
            gproj[:, :, lo : lo + 256] = acc[g, kv, 6:22, 0:16, :].reshape(4, 64, 256).astype(bf16)
            grad_swap(kv + 1, g)

    def unpack(g):
        side_wait(g)
        for piece in range(4):
            lanes = slice(128 * (piece % 2), 128 * (piece % 2) + 128)
            slabs = [
                unpack_columns(*[side_recv[g, n, piece, :, m].astype(f32) for m in range(3)]) for n in range(2)
            ]
            pad[g, piece // 2, :, 16:32, lanes] = jnp.concatenate(slabs, axis=1).astype(bf16)

    def grad_copy(j, g):
        lo = 1024 * j + 256 * g
        half = g % 2
        return remote(
            gproj.at[:, :, lo : lo + 256], b_mate.at[j, half], grad_ss.at[j, half], grad_rs.at[j, half], mate
        )

    def grad_swap(j, g):
        @pl.when(core != g // 2)
        def _():
            grad_copy(j, g).start()

    def left_copy(kind, n):
        return remote(
            at_own.at[kind, n], at_mate.at[kind, n], swap_ss.at[kind, n], swap_rs.at[kind, n], mate
        )

    branch_copies = []
    for half in range(2):
        lo = pl.multiple_of((1 - core) * 512 + 256 * half, 256)
        branch_copies.append(
            remote(branch.at[:, :, pl.ds(lo, 256)], b_mate.at[3, half], grad_ss.at[3, half], grad_rs.at[3, half], mate)
        )

    sbuf = [[ring_bufs[c * 3 + p] for p in range(3)] for c in range(4)]
    rbuf = [[ring_bufs[12 + c * 3 + p] for p in range(3)] for c in range(4)]
    keep = [[ring_bufs[24 + c * 3 + p] for p in range(3)] for c in range(4)]
    part = [[ring_bufs[36 + c * 3 + p] for p in range(3)] for c in range(4)]

    def ring_copy(c, p, s):
        by = 1 if s in (0, 2, 4) else -1
        return remote(
            sbuf[c][p].at[s], rbuf[c][p].at[s],
            ring_ss.at[c, p, s], ring_rs.at[c, p, s], neighbour(CHUNK_AXES[c][p], by),
        )

    def ring_block(c, p, by):
        axis = CHUNK_AXES[c][p]
        j = (axis_coord(axis) + by + 4) % 4
        if p > 0:
            return part[c][p - 1][pick(None, CHUNK_AXES[c][p:], axis, j)].reshape(256 >> (2 * p), 512)
        kind = 1 if c == 3 else 0
        index = (kind,) + pick(None, "xyz", axis, j)
        left_own = at_own[index].reshape(256, 256)
        left_mate = at_mate[index].reshape(256, 256)
        base = 0 if c == 3 else 1024 * c
        columns = pl.ds(pl.multiple_of(base + 512 * core, 512), 512)
        right_own = (branch if c == 3 else gproj)[:, :, columns].reshape(256, 512)
        right_mate = jnp.concatenate([b_mate[c, 0].reshape(256, 256), b_mate[c, 1].reshape(256, 256)], axis=1)
        return dot_nn(left_own, right_own) + dot_nn(left_mate, right_mate)

    def ring_start(c, p):
        value = ring_block(c, p, 2)
        sbuf[c][p][0] = value[:, :256].astype(bf16)
        ring_copy(c, p, 0).start()
        sbuf[c][p][1] = value[:, 256:].astype(bf16)
        ring_copy(c, p, 1).start()
        value = ring_block(c, p, 1)
        sbuf[c][p][2] = value[:, 256:].astype(bf16)
        ring_copy(c, p, 2).start()
        keep[c][p][0] = value[:, :256]
        value = ring_block(c, p, -1)
        sbuf[c][p][3] = value[:, :256].astype(bf16)
        ring_copy(c, p, 3).start()
        keep[c][p][1] = value[:, 256:]
        part[c][p][...] = ring_block(c, p, 0).reshape(part[c][p].shape)

    def ring_relay(c, p):
        for s in (0, 1):
            ring_copy(c, p, s).wait_recv()
            sbuf[c][p][4 + s] = (keep[c][p][s] + rbuf[c][p][s].astype(f32)).astype(bf16)
            ring_copy(c, p, 4 + s).start()

    def ring_finish(c, p):
        for s in (2, 3, 4, 5):
            ring_copy(c, p, s).wait_recv()
        shape = part[c][p].shape[:-1] + (256,)
        first = rbuf[c][p][3].astype(f32) + rbuf[c][p][4].astype(f32)
        second = rbuf[c][p][2].astype(f32) + rbuf[c][p][5].astype(f32)
        part[c][p][..., :256] += first.reshape(shape)
        part[c][p][..., 256:] += second.reshape(shape)

    def swap_wait(c):
        for half in range(2):
            grad_copy(c, half).wait_recv()

    def attend_all(g):
        unpack(g)
        attend(g)
        start_back(g)
        grad_swap(0, g)
        columns = slice(256 * g, 256 * g + 256)
        at_own[1, g] = attended[:, :, columns].reshape(256, 256).T.reshape(2, 4, 2, 16, 256)
        left_copy(1, g).start()

    for n in range(4):
        columns = slice(256 * n, 256 * n + 256)
        at_own[0, n] = normed[:, columns].T.reshape(2, 4, 2, 16, 256)
        left_copy(0, n).start()
    for copy in branch_copies:
        copy.start()
    prepare(0)
    prepare(1)
    side_forward(0)
    prepare(2)
    side_forward(1)
    query_load.wait()
    upstream_load.wait()
    attend_all(0)
    prepare(3)
    side_forward(2)
    attend_all(1)
    back_forward(0)
    side_forward(3)
    attend_all(2)
    back_forward(1)
    start_up(0)
    attend_all(3)
    back_forward(2)
    start_up(1)
    finish(0)
    for n in range(4):
        left_copy(0, n).wait_recv()
        left_copy(1, n).wait_recv()
    for copy in branch_copies:
        copy.wait_recv()
    swap_wait(0)
    ring_start(0, 0)
    back_forward(3)
    start_up(2)
    finish(1)
    ring_start(3, 0)
    start_up(3)
    finish(2)
    ring_relay(0, 0)
    finish(3)
    for c in (1, 2):
        swap_wait(c)
        ring_start(c, 0)
    ring_relay(3, 0)
    weight_load.wait()
    flat = attended[...].reshape(256, 1024)
    for n in range(4):
        columns = slice(256 * n, 256 * n + 256)
        product = dot_nn(flat, weight_vmem[:, 3072 + 256 * n : 3328 + 256 * n])
        block_output[:, columns] = (tokens[:, columns].astype(f32) + tissue[...] * product).astype(bf16)
    ring_relay(1, 0)
    ring_relay(2, 0)
    flat = gproj[...].reshape(256, 3072)
    for n in range(4):
        rows = slice(256 * n, 256 * n + 256)
        grad_normed[:, rows] = dot_nt(flat, weight_vmem[rows, 0:3072])
    for c in (0, 3, 1, 2):
        ring_finish(c, 0)
        ring_start(c, 1)
    for c in (0, 3, 1, 2):
        ring_relay(c, 1)

    def norm_rows(n, carry):
        rows = pl.ds(pl.multiple_of(64 * n, 64), 64)
        wide = tokens[rows, :].astype(f32)
        centred = wide - jnp.mean(wide, axis=1, keepdims=True)
        inverse = lax.rsqrt(jnp.mean(centred * centred, axis=1, keepdims=True) + EPSILON)
        normalized = centred * inverse
        scaled = grad_normed[rows, :] * gain[...]
        first_mean = jnp.mean(scaled, axis=1, keepdims=True)
        second_mean = jnp.mean(scaled * normalized, axis=1, keepdims=True)
        grad = cotangent[rows, :].astype(f32) + inverse * (scaled - first_mean - normalized * second_mean)
        input_grad[rows, :] = grad.astype(bf16)
        return carry

    lax.fori_loop(0, 4, norm_rows, 0)
    for c in (0, 3, 1, 2):
        ring_finish(c, 1)
        ring_start(c, 2)
    for c in (0, 3, 1, 2):
        ring_relay(c, 2)
    for c in (0, 3, 1, 2):
        ring_finish(c, 2)
        value = part[c][2][...] * inv_root
        mine = jnp.where(core == 0, value[:8], value[8:])
        theirs = jnp.where(core == 0, value[8:], value[:8])
        last_send[c] = theirs
        final_copy = remote(last_send.at[c], last_recv.at[c], swap_ss.at[2, c], swap_rs.at[2, c], mate)
        final_copy.start()
        offset = pl.multiple_of(1024 * c + 512 * core, 512)
        weight_grads[:, pl.ds(offset, 512)] = mine
    for c in (0, 3, 1, 2):
        final_copy = remote(last_send.at[c], last_recv.at[c], swap_ss.at[2, c], swap_rs.at[2, c], mate)
        final_copy.wait_recv()
        offset = pl.multiple_of(1024 * c + 512 * (1 - core), 512)
        weight_grads[:, pl.ds(offset, 512)] = last_recv[c]
        final_copy.wait_send()
        for p in range(3):
            for s in range(6):
                ring_copy(c, p, s).wait_send()
    for n in range(4):
        left_copy(0, n).wait_send()
        left_copy(1, n).wait_send()
        drain(n)
        for j in range(3):
            @pl.when(core != n // 2)
            def _(j=j, n=n):
                grad_copy(j, n).wait_send()
    for copy in branch_copies:
        copy.wait_send()


def sublayer(projected, grad_attn, weights, normed, branch, tokens, cotangent, tissue, gain, inv_root):
    bf16, f32 = jnp.bfloat16, jnp.float32
    dma = pltpu.SemaphoreType.DMA
    any_space = pl.BlockSpec(memory_space=pl.ANY)
    vmem = pl.BlockSpec(memory_space=pltpu.VMEM)
    ring = []
    for _ in range(2):
        for c in range(4):
            for p in range(3):
                ring.append(pltpu.VMEM((6, 256 >> (2 * p), 256), bf16))
    for c in range(4):
        for p in range(3):
            ring.append(pltpu.VMEM((2, 256 >> (2 * p), 256), f32))
    for c in range(4):
        for p in range(3):
            ring.append(pltpu.VMEM(row_dims(CHUNK_AXES[c][p + 1 :]) + (16, 512), f32))
    slab = pltpu.VMEM((4, 2, 4, 7, 3, 8, 128), bf16)
    relay = pltpu.VMEM((4, 4, 7, 3, 8, 128), bf16)
    return pl.pallas_call(
        functools.partial(sublayer_kernel, inv_root),
        out_shape=(
            jax.ShapeDtypeStruct((256, 1024), bf16),
            jax.ShapeDtypeStruct((256, 1024), bf16),
            jax.ShapeDtypeStruct((8, 4096), f32),
        ),
        in_specs=[any_space] * 4 + [vmem] * 6,
        out_specs=(vmem,) * 3,
        scratch_shapes=[
            pltpu.VMEM((4, 64, 1024), bf16),
            pltpu.VMEM((4, 64, 3072), bf16),
            pltpu.VMEM((1024, 4096), bf16),
            pltpu.VMEM((256, 1024), f32),
            pltpu.VMEM((4, 2, 28, 32, 256), bf16),
            pltpu.VMEM((4, 64, 1024), bf16),
            pltpu.VMEM((4, 64, 1024), bf16),
            pltpu.VMEM((4, 512, 256), f32),
            pltpu.VMEM((4, 2, 28, 32, 256), f32),
            slab, slab, slab, slab,
            pltpu.VMEM((4, 2, 2, 6, 16, 256), bf16),
            pltpu.VMEM((4, 2, 2, 6, 16, 256), bf16),
            relay, relay,
            pltpu.VMEM((2, 4, 2, 4, 2, 16, 256), bf16),
            pltpu.VMEM((2, 4, 2, 4, 2, 16, 256), bf16),
            pltpu.VMEM((4, 2, 4, 64, 256), bf16),
            pltpu.VMEM((4, 8, 512), f32),
            pltpu.VMEM((4, 8, 512), f32),
            dma((11,)),
        ]
        + [dma((4, 2))] * 4
        + [dma((4,))] * 4
        + [dma((4, 4))] * 8
        + [dma((3, 4))] * 2
        + [dma((4, 2))] * 2
        + [dma((4, 3, 6))] * 2
        + ring,
        compiler_params=pltpu.CompilerParams(
            collective_id=0, has_side_effects=True, vmem_limit_bytes=67043328
        ),
    )(
        projected.reshape(16, 16, 3072),
        projected.reshape(4, 64, 3072),
        grad_attn.reshape(4, 64, 1024),
        weights,
        normed,
        branch.reshape(4, 64, 1024),
        tokens,
        cotangent,
        tissue,
        gain,
    )


def local(tokens, weights, norm_gain, tissue, cotangent):
    model_width = tokens.shape[-1]
    token_count = tokens.shape[1] * tokens.shape[2]
    group_count = lax.axis_size("slide") * lax.axis_size("gy") * lax.axis_size("gx")
    inv_root = 1.0 / math.sqrt(group_count * token_count)
    weight_in = weights[:, : 3 * model_width]
    weight_out = weights[:, 3 * model_width :]
    tokens_float = tokens.reshape(token_count, model_width).astype(jnp.float32)
    row_mean = jnp.mean(tokens_float, axis=-1, keepdims=True)
    centered = tokens_float - row_mean
    variance = jnp.mean(centered * centered, axis=-1, keepdims=True)
    inverse = lax.rsqrt(variance + EPSILON)
    normalized = centered * inverse
    normed = (normalized * norm_gain).astype(jnp.bfloat16)
    projected = jnp.dot(normed, weight_in, preferred_element_type=jnp.float32).astype(jnp.bfloat16)
    tissue_mask = tissue.reshape(token_count, 1).astype(jnp.float32)
    upstream = cotangent.reshape(token_count, model_width).astype(jnp.float32)
    branch_grad = (tissue_mask * upstream).astype(jnp.bfloat16)
    grad_attn = jnp.dot(branch_grad, weight_out.T, preferred_element_type=jnp.float32).astype(
        jnp.bfloat16
    )
    block_output, input_grad, weight_grads = sublayer(
        projected,
        grad_attn,
        weights,
        normed,
        branch_grad,
        tokens.reshape(token_count, model_width),
        cotangent.reshape(token_count, model_width),
        tissue_mask,
        norm_gain.reshape(1, model_width),
        inv_root,
    )
    return (block_output.reshape(tokens.shape), input_grad.reshape(tokens.shape), weight_grads)


def solution(mesh):
    in_specs = (
        P("slide", "gy", "gx", None),
        P(),
        P(),
        P("slide", "gy", "gx"),
        P("slide", "gy", "gx", None),
    )
    out_specs = (
        P("slide", "gy", "gx", None),
        P("slide", "gy", "gx", None),
        P(("slide", "gy", "gx"), None),
    )
    return jax.shard_map(local, mesh=mesh, in_specs=in_specs, out_specs=out_specs, check_vma=False)
```

time: 122 us -> 109 us (0.89)
  Pallas kernels: 95.2 us -> 85.8 us
  matrix products: 17.6 us -> 9.04 us
  local copies, waits for them, and re-layouts: 0.93 us -> 6.42 us
    pallas_call x2 -> x1, Pallas kernels: 95.2 us -> 85.8 us  [sublayer(): pl.pallas_call(functools.partial(sublayer_kernel, inv_root), out_shape=(j...]
    dot_general x2 -> x0, matrix products: 8.51 us -> none  [the longest x1 5.36 us: local(): jnp.dot(grad_projected, weight_in.T, preferred_element_type=jnp.float32)]
    unnamed x15 -> x5, local copies, waits for them, and re-layouts: 0.69 us -> 5.33 us
    convert_element_type x1 -> x0, other arithmetic: 1.25 us -> none  [local(): (upstream + inverse * (scaled - first_mean - normalized * second_mean)).a...]
where the time goes in v3:
time: 109 us
  Pallas kernels  85.8 us (79%)
  matrix products  9.04 us (8%)
  other arithmetic  6.75 us (6%)
  local copies, waits for them, and re-layouts  6.42 us (6%)
    pallas_call x1, Pallas kernels, sublayer(): pl.pallas_call(functools.partial(sublayer_kernel, inv_root), out_shape=(j...  85.8 us
    dot_general x1, matrix products, local(): jnp.dot(normed, weight_in, preferred_element_type=jnp.float32)  5.73 us
    unnamed x5, local copies, waits for them, and re-layouts  5.33 us
    dot_general x1, matrix products, local(): jnp.dot(branch_grad, weight_out.T, preferred_element_type=jnp.float32)  3.31 us
    convert_element_type x1, other arithmetic, local(): branch_grad = (tissue_mask * upstream).astype(jnp.bfloat16)  2.2 us

profile of v3, /device:TPU:1, one launch (start us, length us, event | category | flops | bytes accessed | tf_op | source)
XLA Modules:
  0.0 108.7 jit_solution(15413820966471218158)
XLA Ops:
  0.6 0.7 convert_element_type.44
  1.3 0.1 convert_element_type.45
  1.4 0.1 convert_element_type.49
  1.5 1.2 %convert_reduce_fusion = f32[16,16]{1,0:T(8,128)S(1)} fusion(bf16[1,16,16,1024]{3,2,1,0:T(8,128)(2,1)} %param.5), kind=kLoop, calls=%fused_computation.6 | loop fusion | flops 524032 | bytes 525312 | tf_op jit(solution)/shard_map/reduce_sum | solution.py:702
  2.7 0.1 div.9
  2.8 1.3 %fusion.11 = f32[16,16]{1,0:T(8,128)S(1)} fusion(bf16[1,16,16,1024]{3,2,1,0:T(8,128)(2,1)} %param.5, f32[16,16]{1,0:T(8,128)S(1)} %broadcast_multiply_fusion), kind=kLoop, calls=%fused_computation.9 | loop fusion | flops 1048320 | bytes 526336 | tf_op jit(solution)/shard_map/reduce_sum | solution.py:704
  4.1 0.1 rsqrt.12
  4.2 0.8 convert_element_type.55.tissue
  4.9 1.3 %multiply_convert_fusion.1.normed = bf16[256,1024]{1,0:T(8,128)(2,1)S(1)} fusion(f32[1024]{0:T(1024)} %param.7, f32[256]{0:T(256)S(1)} %rsqrt.12, f32[256]{0:T(256)S(1)} %div.9, bf16[1,16,16,1024]{3,2,1,0:T(8,128)(2,1)} %param.5), kind=kLoop, calls=%fused_computation.13 | loop fusion | flops 1310720 | bytes 1054720 | tf_op jit(solution)/shard_map/convert_element_type | solution.py:707
  6.3 0.0 copy-start
  6.3 2.2 %fusion.12.branch = bf16[4,64,1024]{2,1,0:T(8,128)(2,1)} fusion(bf16[4,64,1024]{2,1,0:T(8,128)(2,1)} %bitcast.15, f32[4,64]{1,0:T(4,128)S(1)} %convert_element_type.49), kind=kLoop, calls=%fused_computation.11 | loop fusion | flops 786432 | bytes 1049600 | tf_op jit(solution)/shard_map/convert_element_type | solution.py:711
  8.5 3.3 %fusion.7 = bf16[256,1024]{1,0:T(8,128)(2,1)} fusion(bf16[1024,4096]{1,0:T(8,128)(2,1)} %weights.1, bf16[256,1024]{1,0:T(8,128)(2,1)} %bitcast.16, f32[256]{0:T(256)S(1)} %convert_element_type.45), kind=kOutput, calls=%fused_computation.7 | convolution fusion | flops 537919488 | bytes 3146752 | tf_op jit(solution)/shard_map/dot_general | solution.py:712
  11.8 5.7 %fusion.2 = bf16[256,3072]{1,0:T(8,128)(2,1)} fusion(bf16[256,1024]{1,0:T(8,128)(2,1)S(1)} %multiply_convert_fusion.1.normed, bf16[1024,4096]{1,0:T(8,128)(2,1)} %weights.1), kind=kOutput, calls=%fused_computation.2 | convolution fusion | flops 1611399168 | bytes 8388608 | tf_op jit(solution)/shard_map/dot_general | solution.py:708
  17.6 0.0 copy-done
  17.6 85.8 %shard_map.76 = (bf16[256,1024]{1,0:T(8,128)(2,1)}, bf16[256,1024]{1,0:T(8,128)(2,1)}, f32[8,4096]{1,0:T(8,128)}) custom-call(bf16[16,16,3072]{2,1,0:T(8,128)(2,1)} %bitcast.13, bf16[4,64,3072]{2,1,0:T(8,128)(2,1)} %bitcast.14, bf16[4,64,1024]{2,1,0:T(8,128)(2,1)} %bitcast.20, bf16[1024,4096]{1,0:T(8,128)(2,1)} %weights.1, bf16[256,1024]{1,0:T(8,128)(2,1)} %copy-done, ...), custom_call_target="tpu_custom_call" | custom-call | tf_op jit(solution)/shard_map/pallas_call | solution.py:640
  103.4 1.9 %copy.12 = bf16[1,16,16,1024]{3,2,1,0:T(8,128)(2,1)} copy(bf16[1,16,16,1024]{3,2,1,0:T(8,128)(2,1)} %bitcast.19) | data formatting | bytes 1048576
  105.3 1.9 %copy.13 = bf16[1,16,16,1024]{3,2,1,0:T(8,128)(2,1)} copy(bf16[1,16,16,1024]{3,2,1,0:T(8,128)(2,1)} %bitcast.18) | data formatting | bytes 1048576
  107.2 1.6 %copy.14 = f32[8,4096]{1,0:T(8,128)} copy(f32[8,4096]{1,0:T(8,128)} %get-tuple-element.14) | data formatting | bytes 262144
  (2 shorter events, 0.0 us)
Async XLA Ops:
  6.3 11.3 %copy-start = (bf16[256,1024]{1,0:T(8,128)(2,1)}, bf16[256,1024]{1,0:T(8,128)(2,1)S(1)}, u32[]{:S(2)}) copy-start(bf16[256,1024]{1,0:T(8,128)(2,1)S(1)} %multiply_convert_fusion.1.normed) | copy-start | bytes 1572868

commit v4 on v3

--- a/solution.py
+++ b/solution.py
@@ -128,9 +128,9 @@
 
 def sublayer_kernel(
     inv_root,
-    projected, projected_rows, grad_attn, weights, normed, branch, tokens, cotangent, tissue, gain,
+    weights, tokens, cotangent, tissue, gain,
     block_output, input_grad, weight_grads,
-    attended, gproj, weight_vmem, grad_normed,
+    normed, branch, mask, attended, gproj, weight_vmem, grad_normed,
     pad, queries, upstream, bias, acc,
     side_send, side_recv, back_send, back_recv, rows_send, rows_recv, side_relay, back_relay,
     at_own, at_mate, b_mate, last_send, last_recv,
@@ -161,25 +161,39 @@
     loads = []
     for g in range(4):
         for kv in range(2):
-            lo = 1024 * (kv + 1) + 256 * g
+            columns = slice(1024 * (kv + 1) + 256 * g, 1024 * (kv + 1) + 256 * g + 256)
             loads.append(
                 pltpu.make_async_copy(
-                    projected.at[:, :, lo : lo + 256], pad.at[g, kv, 6:22, 0:16, :], load_sem.at[2 * g + kv]
+                    weights.at[:, columns], weight_vmem.at[:, columns], load_sem.at[2 * g + kv]
                 )
             )
-            loads[-1].start()
-    query_load = pltpu.make_async_copy(projected_rows.at[:, :, 0:1024], queries, load_sem.at[8])
-    query_load.start()
-    upstream_load = pltpu.make_async_copy(grad_attn, upstream, load_sem.at[9])
-    upstream_load.start()
-    weight_load = pltpu.make_async_copy(weights, weight_vmem, load_sem.at[10])
-    weight_load.start()
+    for n, columns in ((8, slice(0, 1024)), (9, slice(3072, 4096))):
+        loads.append(
+            pltpu.make_async_copy(weights.at[:, columns], weight_vmem.at[:, columns], load_sem.at[n])
+        )
+    for load in loads:
+        load.start()
 
     barrier = pltpu.get_barrier_semaphore()
     greeted = [mate, (slide, (gy + 7) % 8, gx), (slide, (gy + 1) % 8, gx), opposite(1), opposite(-1)]
     greeted += [neighbour(axis, by) for axis in "xyz" for by in (1, -1)]
     for dev in greeted:
         pl.semaphore_signal(barrier, inc=1, device_id=dev, device_id_type=pl.DeviceIdType.MESH)
+    flags = tissue[...].astype(f32)
+    place = lax.broadcasted_iota(jnp.int32, (16, 16, 16), 1) == lax.broadcasted_iota(jnp.int32, (16, 16, 16), 2)
+    picked = jnp.where(place, jnp.broadcast_to(flags[:, None, :], (16, 16, 16)), 0.0)
+    mask[...] = jnp.sum(picked, axis=2, keepdims=True).reshape(256, 1)
+
+    def norm_forward(n, carry):
+        rows = pl.ds(pl.multiple_of(64 * n, 64), 64)
+        wide = tokens[rows, :].astype(f32)
+        centred = wide - jnp.mean(wide, axis=1, keepdims=True)
+        inverse = lax.rsqrt(jnp.mean(centred * centred, axis=1, keepdims=True) + EPSILON)
+        normed[rows, :] = (centred * inverse * gain[...]).astype(bf16)
+        branch[n] = (mask[rows, :] * cotangent[rows, :].astype(f32)).astype(bf16)
+        return carry
+
+    lax.fori_loop(0, 4, norm_forward, 0)
     pl.semaphore_wait(barrier, len(greeted))
 
     def rows_copy(g, side):
@@ -278,6 +292,9 @@
     for g in range(4):
         for kv in range(2):
             loads[2 * g + kv].wait()
+            columns = slice(1024 * (kv + 1) + 256 * g, 1024 * (kv + 1) + 256 * g + 256)
+            made = dot_nn(normed[...], weight_vmem[:, columns]).astype(bf16)
+            pad[g, kv, 6:22, 0:16, :] = made.reshape(16, 16, 256)
         for side in range(2):
             @pl.when(has_along[side])
             def _(g=g, side=side):
@@ -336,7 +353,7 @@
         def block(b, carry):
             keys = pad[g, 0, pl.ds(4 * b, 16)].reshape(512, 256)
             values = pad[g, 1, pl.ds(4 * b, 16)].reshape(512, 256)
-            query = queries[b, :, columns] * jnp.asarray(0.125, bf16)
+            query = queries[b, :, columns]
             grad = upstream[b, :, columns]
             query_heads = jnp.concatenate([query] * 4, axis=0) * head_mask
             grad_heads = jnp.concatenate([grad] * 4, axis=0) * head_mask
@@ -512,13 +529,22 @@
         left_copy(0, n).start()
     for copy in branch_copies:
         copy.start()
+    loads[8].wait()
+    for n in range(4):
+        columns = slice(256 * n, 256 * n + 256)
+        made = dot_nn(normed[...], weight_vmem[:, columns]).astype(bf16) * jnp.asarray(0.125, bf16)
+        queries[:, :, columns] = made.reshape(4, 64, 256)
+    loads[9].wait()
+    flat = branch[...].reshape(256, 1024)
+    for n in range(4):
+        columns = slice(256 * n, 256 * n + 256)
+        made = dot_nt(flat, weight_vmem[columns, 3072:4096]).astype(bf16)
+        upstream[:, :, columns] = made.reshape(4, 64, 256)
     prepare(0)
     prepare(1)
     side_forward(0)
     prepare(2)
     side_forward(1)
-    query_load.wait()
-    upstream_load.wait()
     attend_all(0)
     prepare(3)
     side_forward(2)
@@ -551,12 +577,11 @@
         swap_wait(c)
         ring_start(c, 0)
     ring_relay(3, 0)
-    weight_load.wait()
     flat = attended[...].reshape(256, 1024)
     for n in range(4):
         columns = slice(256 * n, 256 * n + 256)
         product = dot_nn(flat, weight_vmem[:, 3072 + 256 * n : 3328 + 256 * n])
-        block_output[:, columns] = (tokens[:, columns].astype(f32) + tissue[...] * product).astype(bf16)
+        block_output[:, columns] = (tokens[:, columns].astype(f32) + mask[...] * product).astype(bf16)
     ring_relay(1, 0)
     ring_relay(2, 0)
     flat = gproj[...].reshape(256, 3072)
@@ -619,7 +644,7 @@
         copy.wait_send()
 
 
-def sublayer(projected, grad_attn, weights, normed, branch, tokens, cotangent, tissue, gain, inv_root):
+def sublayer(weights, tokens, cotangent, tissue, gain, inv_root):
     bf16, f32 = jnp.bfloat16, jnp.float32
     dma = pltpu.SemaphoreType.DMA
     any_space = pl.BlockSpec(memory_space=pl.ANY)
@@ -644,9 +669,12 @@
             jax.ShapeDtypeStruct((256, 1024), bf16),
             jax.ShapeDtypeStruct((8, 4096), f32),
         ),
-        in_specs=[any_space] * 4 + [vmem] * 6,
+        in_specs=[any_space] + [vmem] * 4,
         out_specs=(vmem,) * 3,
         scratch_shapes=[
+            pltpu.VMEM((256, 1024), bf16),
+            pltpu.VMEM((4, 64, 1024), bf16),
+            pltpu.VMEM((256, 1), f32),
             pltpu.VMEM((4, 64, 1024), bf16),
             pltpu.VMEM((4, 64, 3072), bf16),
             pltpu.VMEM((1024, 4096), bf16),
@@ -665,7 +693,7 @@
             pltpu.VMEM((4, 2, 4, 64, 256), bf16),
             pltpu.VMEM((4, 8, 512), f32),
             pltpu.VMEM((4, 8, 512), f32),
-            dma((11,)),
+            dma((10,)),
         ]
         + [dma((4, 2))] * 4
         + [dma((4,))] * 4
@@ -677,18 +705,7 @@
         compiler_params=pltpu.CompilerParams(
             collective_id=0, has_side_effects=True, vmem_limit_bytes=67043328
         ),
-    )(
-        projected.reshape(16, 16, 3072),
-        projected.reshape(4, 64, 3072),
-        grad_attn.reshape(4, 64, 1024),
-        weights,
-        normed,
-        branch.reshape(4, 64, 1024),
-        tokens,
-        cotangent,
-        tissue,
-        gain,
-    )
+    )(weights, tokens, cotangent, tissue, gain)
 
 
 def local(tokens, weights, norm_gain, tissue, cotangent):
@@ -696,31 +713,11 @@
     token_count = tokens.shape[1] * tokens.shape[2]
     group_count = lax.axis_size("slide") * lax.axis_size("gy") * lax.axis_size("gx")
     inv_root = 1.0 / math.sqrt(group_count * token_count)
-    weight_in = weights[:, : 3 * model_width]
-    weight_out = weights[:, 3 * model_width :]
-    tokens_float = tokens.reshape(token_count, model_width).astype(jnp.float32)
-    row_mean = jnp.mean(tokens_float, axis=-1, keepdims=True)
-    centered = tokens_float - row_mean
-    variance = jnp.mean(centered * centered, axis=-1, keepdims=True)
-    inverse = lax.rsqrt(variance + EPSILON)
-    normalized = centered * inverse
-    normed = (normalized * norm_gain).astype(jnp.bfloat16)
-    projected = jnp.dot(normed, weight_in, preferred_element_type=jnp.float32).astype(jnp.bfloat16)
-    tissue_mask = tissue.reshape(token_count, 1).astype(jnp.float32)
-    upstream = cotangent.reshape(token_count, model_width).astype(jnp.float32)
-    branch_grad = (tissue_mask * upstream).astype(jnp.bfloat16)
-    grad_attn = jnp.dot(branch_grad, weight_out.T, preferred_element_type=jnp.float32).astype(
-        jnp.bfloat16
-    )
     block_output, input_grad, weight_grads = sublayer(
-        projected,
-        grad_attn,
         weights,
-        normed,
-        branch_grad,
         tokens.reshape(token_count, model_width),
         cotangent.reshape(token_count, model_width),
-        tissue_mask,
+        tissue[0],
         norm_gain.reshape(1, model_width),
         inv_root,
     )

time: 109 us -> 92.6 us (0.85)
  matrix products: 9.04 us -> 0 us
  other arithmetic: 6.75 us -> 0 us
    dot_general x2 -> x0, matrix products: 9.04 us -> none  [the longest x1 5.73 us: local(): jnp.dot(normed, weight_in, preferred_element_type=jnp.float32)]
    convert_element_type x3 -> x0, other arithmetic: 4.24 us -> none  [the longest x1 2.2 us: local(): branch_grad = (tissue_mask * upstream).astype(jnp.bfloat16)]
    reduce_sum x2 -> x0, other arithmetic: 2.49 us -> none  [the longest x1 1.31 us: local(): variance = jnp.mean(centered * centered, axis=-1, keepdims=True)]
    unnamed x5 -> x3, local copies, waits for them, and re-layouts: 5.33 us -> 5.33 us
where the time goes in v4:
time: 92.6 us; the launch traced here: 92.3 us
  Pallas kernels  86.4 us (93%)
  local copies, waits for them, and re-layouts  5.33 us (6%)
    pallas_call x1, Pallas kernels, sublayer(): pl.pallas_call(functools.partial(sublayer_kernel, inv_root), out_shape=(j...  86.4 us
    unnamed x3, local copies, waits for them, and re-layouts  5.33 us

profile of v4, /device:TPU:1, one launch (start us, length us, event | category | flops | bytes accessed | tf_op | source)
XLA Modules:
  0.0 92.3 jit_solution(15870227965185255321)
XLA Ops:
  0.6 86.4 %shard_map.76 = (bf16[256,1024]{1,0:T(8,128)(2,1)}, bf16[256,1024]{1,0:T(8,128)(2,1)}, f32[8,4096]{1,0:T(8,128)}) custom-call(bf16[1024,4096]{1,0:T(8,128)(2,1)} %weights.1, bf16[256,1024]{1,0:T(8,128)(2,1)} %bitcast.6, bf16[256,1024]{1,0:T(8,128)(2,1)} %bitcast.7, s32[16,16]{1,0:T(8,128)} %bitcast.10, f32[1,1024]{1,0:T(1,128)} %bitcast.11), custom_call_target="tpu_custom_call" | custom-call | tf_op jit(solution)/shard_map/pallas_call | solution.py:665
  87.0 1.9 %copy.11 = bf16[1,16,16,1024]{3,2,1,0:T(8,128)(2,1)} copy(bf16[1,16,16,1024]{3,2,1,0:T(8,128)(2,1)} %bitcast.9) | data formatting | bytes 1048576
  88.9 1.9 %copy.12 = bf16[1,16,16,1024]{3,2,1,0:T(8,128)(2,1)} copy(bf16[1,16,16,1024]{3,2,1,0:T(8,128)(2,1)} %bitcast.8) | data formatting | bytes 1048576
  90.8 1.6 %copy.13 = f32[8,4096]{1,0:T(8,128)} copy(f32[8,4096]{1,0:T(8,128)} %get-tuple-element.14) | data formatting | bytes 262144

commit v5 on v4

--- a/solution.py
+++ b/solution.py
@@ -11,9 +11,8 @@
 EPSILON = 1e-06
 
 
-LOADED_UP = 0
-LOADED_DOWN = 3
-CHUNK_AXES = ("xyz", "yzx", "zxy", "xzy")
+DIRECT_FROM = 1
+CHUNK_AXES = ("xyz", "yzx", "xzy", "zyx")
 
 
 def coords():
@@ -132,10 +131,10 @@
     block_output, input_grad, weight_grads,
     normed, branch, mask, attended, gproj, weight_vmem, grad_normed,
     pad, queries, upstream, bias, acc,
-    side_send, side_recv, back_send, back_recv, rows_send, rows_recv, side_relay, back_relay,
+    side_send, side_recv, back_send, back_recv, rows_send, rows_recv,
     at_own, at_mate, b_mate, last_send, last_recv,
     load_sem, rows_ss, rows_rs, up_ss, up_rs, side_ss, side_rs, back_ss, back_rs,
-    far_ss, far_rs, far_relay_ss, far_relay_rs, farb_ss, farb_rs, farb_relay_ss, farb_relay_rs,
+    far_ss, far_rs, farb_ss, farb_rs,
     swap_ss, swap_rs, grad_ss, grad_rs, ring_ss, ring_rs,
     *ring_bufs,
 ):
@@ -149,14 +148,8 @@
     outer = (gx == 0) | (gx == 3)
     inner = jnp.logical_not(outer)
     mate = mate_id()
-    signs = (1, jnp.where(y == LOADED_UP, -1, 1), jnp.where(y == LOADED_DOWN, 1, -1), -1)
-
-    def opposite(by):
-        other = (z + by + 4) % 4
-        high = other // 2
-        return (slide, (other % 2) * 4 + y, jnp.where(outer, high + 1, 3 * high))
-
-    across = [opposite(sign) for sign in signs]
+    high = 1 - z // 2
+    far = (slide, gy, jnp.where(outer, 3 * high, high + 1))
 
     loads = []
     for g in range(4):
@@ -175,8 +168,8 @@
         load.start()
 
     barrier = pltpu.get_barrier_semaphore()
-    greeted = [mate, (slide, (gy + 7) % 8, gx), (slide, (gy + 1) % 8, gx), opposite(1), opposite(-1)]
-    greeted += [neighbour(axis, by) for axis in "xyz" for by in (1, -1)]
+    greeted = [mate, (slide, (gy + 7) % 8, gx), (slide, (gy + 1) % 8, gx), far]
+    greeted += [neighbour(axis, by) for axis in "xyz" for by in (1, -1, 2)]
     for dev in greeted:
         pl.semaphore_signal(barrier, inc=1, device_id=dev, device_id_type=pl.DeviceIdType.MESH)
     flags = tissue[...].astype(f32)
@@ -207,76 +200,48 @@
     def mate_copy(g, sent, got, ss, rs):
         return remote(sent.at[g, 1 - core], got.at[g, 1 - core], ss.at[g], rs.at[g], mate)
 
-    def far_copy(g, kv, sent, relay, ss, rs):
-        return remote(sent.at[g, core, kv], relay.at[g, kv], ss.at[g, kv], rs.at[g, kv], across[kv])
-
-    def relay_copy(g, kv, relay, got, ss, rs):
-        source = (z - signs[kv] + 4) % 4
-        return remote(
-            relay.at[g, kv], got.at[g, 1 - source // 2, kv], ss.at[g, kv], rs.at[g, kv], across[kv]
-        )
+    def far_copy(g, sent, got, ss, rs):
+        return remote(sent.at[g, core], got.at[g, core], ss.at[g], rs.at[g], far)
+
+    side_set = (side_send, side_recv)
+    back_set = (back_send, back_recv)
 
     def side_start(g):
-        mate_copy(g, side_send, side_recv, side_ss, side_rs).start()
+        mate_copy(g, *side_set, side_ss, side_rs).start()
 
         @pl.when(inner)
         def _():
-            for kv in range(4):
-                far_copy(g, kv, side_send, side_relay, far_ss, far_rs).start()
-
-    def side_forward(g):
-        @pl.when(outer)
-        def _():
-            for kv in range(4):
-                far_copy(g, kv, side_send, side_relay, far_ss, far_rs).wait_recv()
-                relay_copy(g, kv, side_relay, side_recv, far_relay_ss, far_relay_rs).start()
+            far_copy(g, *side_set, far_ss, far_rs).start()
 
     def side_wait(g):
-        mate_copy(g, side_send, side_recv, side_ss, side_rs).wait_recv()
+        mate_copy(g, *side_set, side_ss, side_rs).wait_recv()
 
         @pl.when(inner)
         def _():
-            for kv in range(4):
-                relay_copy(g, kv, side_relay, side_recv, far_relay_ss, far_relay_rs).wait_recv()
+            far_copy(g, *side_set, far_ss, far_rs).wait_recv()
 
     def back_start(g):
-        mate_copy(g, back_send, back_recv, back_ss, back_rs).start()
+        mate_copy(g, *back_set, back_ss, back_rs).start()
 
         @pl.when(inner)
         def _():
-            for kv in range(4):
-                far_copy(g, kv, back_send, back_relay, farb_ss, farb_rs).start()
-
-    def back_forward(g):
-        @pl.when(outer)
-        def _():
-            for kv in range(4):
-                far_copy(g, kv, back_send, back_relay, farb_ss, farb_rs).wait_recv()
-                relay_copy(g, kv, back_relay, back_recv, farb_relay_ss, farb_relay_rs).start()
+            far_copy(g, *back_set, farb_ss, farb_rs).start()
 
     def back_wait(g):
-        mate_copy(g, back_send, back_recv, back_ss, back_rs).wait_recv()
+        mate_copy(g, *back_set, back_ss, back_rs).wait_recv()
 
         @pl.when(inner)
         def _():
-            for kv in range(4):
-                relay_copy(g, kv, back_relay, back_recv, farb_relay_ss, farb_relay_rs).wait_recv()
+            far_copy(g, *back_set, farb_ss, farb_rs).wait_recv()
 
     def drain(g):
-        mate_copy(g, side_send, side_recv, side_ss, side_rs).wait_send()
-        mate_copy(g, back_send, back_recv, back_ss, back_rs).wait_send()
+        mate_copy(g, *side_set, side_ss, side_rs).wait_send()
+        mate_copy(g, *back_set, back_ss, back_rs).wait_send()
 
         @pl.when(inner)
         def _():
-            for kv in range(4):
-                far_copy(g, kv, side_send, side_relay, far_ss, far_rs).wait_send()
-                far_copy(g, kv, back_send, back_relay, farb_ss, farb_rs).wait_send()
-
-        @pl.when(outer)
-        def _():
-            for kv in range(4):
-                relay_copy(g, kv, side_relay, side_recv, far_relay_ss, far_relay_rs).wait_send()
-                relay_copy(g, kv, back_relay, back_recv, farb_relay_ss, farb_relay_rs).wait_send()
+            far_copy(g, *side_set, far_ss, far_rs).wait_send()
+            far_copy(g, *back_set, farb_ss, farb_rs).wait_send()
 
         for side in range(2):
             @pl.when(has_along[side])
@@ -459,6 +424,8 @@
 
     def ring_copy(c, p, s):
         by = 1 if s in (0, 2, 4) else -1
+        if p >= DIRECT_FROM and s < 2:
+            by = 2
         return remote(
             sbuf[c][p].at[s], rbuf[c][p].at[s],
             ring_ss.at[c, p, s], ring_rs.at[c, p, s], neighbour(CHUNK_AXES[c][p], by),
@@ -488,14 +455,24 @@
         value = ring_block(c, p, 1)
         sbuf[c][p][2] = value[:, 256:].astype(bf16)
         ring_copy(c, p, 2).start()
-        keep[c][p][0] = value[:, :256]
+        if p >= DIRECT_FROM:
+            sbuf[c][p][4] = value[:, :256].astype(bf16)
+            ring_copy(c, p, 4).start()
+        else:
+            keep[c][p][0] = value[:, :256]
         value = ring_block(c, p, -1)
         sbuf[c][p][3] = value[:, :256].astype(bf16)
         ring_copy(c, p, 3).start()
-        keep[c][p][1] = value[:, 256:]
+        if p >= DIRECT_FROM:
+            sbuf[c][p][5] = value[:, 256:].astype(bf16)
+            ring_copy(c, p, 5).start()
+        else:
+            keep[c][p][1] = value[:, 256:]
         part[c][p][...] = ring_block(c, p, 0).reshape(part[c][p].shape)
 
     def ring_relay(c, p):
+        if p >= DIRECT_FROM:
+            return
         for s in (0, 1):
             ring_copy(c, p, s).wait_recv()
             sbuf[c][p][4 + s] = (keep[c][p][s] + rbuf[c][p][s].astype(f32)).astype(bf16)
@@ -507,6 +484,11 @@
         shape = part[c][p].shape[:-1] + (256,)
         first = rbuf[c][p][3].astype(f32) + rbuf[c][p][4].astype(f32)
         second = rbuf[c][p][2].astype(f32) + rbuf[c][p][5].astype(f32)
+        if p >= DIRECT_FROM:
+            ring_copy(c, p, 0).wait_recv()
+            ring_copy(c, p, 1).wait_recv()
+            first = first + rbuf[c][p][0].astype(f32)
+            second = second + rbuf[c][p][1].astype(f32)
         part[c][p][..., :256] += first.reshape(shape)
         part[c][p][..., 256:] += second.reshape(shape)
 
@@ -542,22 +524,17 @@
         upstream[:, :, columns] = made.reshape(4, 64, 256)
     prepare(0)
     prepare(1)
-    side_forward(0)
+    attend_all(0)
     prepare(2)
-    side_forward(1)
-    attend_all(0)
+    attend_all(1)
     prepare(3)
-    side_forward(2)
-    attend_all(1)
-    back_forward(0)
-    side_forward(3)
+    start_up(0)
     attend_all(2)
-    back_forward(1)
-    start_up(0)
-    attend_all(3)
-    back_forward(2)
     start_up(1)
     finish(0)
+    attend_all(3)
+    start_up(2)
+    finish(1)
     for n in range(4):
         left_copy(0, n).wait_recv()
         left_copy(1, n).wait_recv()
@@ -565,12 +542,9 @@
         copy.wait_recv()
     swap_wait(0)
     ring_start(0, 0)
-    back_forward(3)
-    start_up(2)
-    finish(1)
-    ring_start(3, 0)
     start_up(3)
     finish(2)
+    ring_start(3, 0)
     ring_relay(0, 0)
     finish(3)
     for c in (1, 2):
@@ -661,7 +635,6 @@
         for p in range(3):
             ring.append(pltpu.VMEM(row_dims(CHUNK_AXES[c][p + 1 :]) + (16, 512), f32))
     slab = pltpu.VMEM((4, 2, 4, 7, 3, 8, 128), bf16)
-    relay = pltpu.VMEM((4, 4, 7, 3, 8, 128), bf16)
     return pl.pallas_call(
         functools.partial(sublayer_kernel, inv_root),
         out_shape=(
@@ -687,7 +660,6 @@
             slab, slab, slab, slab,
             pltpu.VMEM((4, 2, 2, 6, 16, 256), bf16),
             pltpu.VMEM((4, 2, 2, 6, 16, 256), bf16),
-            relay, relay,
             pltpu.VMEM((2, 4, 2, 4, 2, 16, 256), bf16),
             pltpu.VMEM((2, 4, 2, 4, 2, 16, 256), bf16),
             pltpu.VMEM((4, 2, 4, 64, 256), bf16),
@@ -696,8 +668,7 @@
             dma((10,)),
         ]
         + [dma((4, 2))] * 4
-        + [dma((4,))] * 4
-        + [dma((4, 4))] * 8
+        + [dma((4,))] * 8
         + [dma((3, 4))] * 2
         + [dma((4, 2))] * 2
         + [dma((4, 3, 6))] * 2
@@ -706,6 +677,21 @@
             collective_id=0, has_side_effects=True, vmem_limit_bytes=67043328
         ),
     )(weights, tokens, cotangent, tissue, gain)
+
+
+def place_kernel(*refs):
+    for source, target in zip(refs[:3], refs[3:]):
+        target[...] = source[...]
+
+
+def place(*arrays):
+    vmem = pl.BlockSpec(memory_space=pltpu.VMEM)
+    return pl.pallas_call(
+        place_kernel,
+        out_shape=tuple(jax.ShapeDtypeStruct(a.shape, a.dtype) for a in arrays),
+        in_specs=[vmem] * 3,
+        out_specs=(vmem,) * 3,
+    )(*arrays)
 
 
 def local(tokens, weights, norm_gain, tissue, cotangent):
@@ -721,6 +707,7 @@
         norm_gain.reshape(1, model_width),
         inv_root,
     )
+    block_output, input_grad, weight_grads = place(block_output, input_grad, weight_grads)
     return (block_output.reshape(tokens.shape), input_grad.reshape(tokens.shape), weight_grads)
 
 

time: 92.6 us -> 85.4 us (0.922)
  local copies, waits for them, and re-layouts: 5.33 us -> 0 us
  Pallas kernels: 86.4 us -> 84.5 us
    unnamed x3 -> x0, local copies, waits for them, and re-layouts: 5.33 us -> none
    pallas_call x1, Pallas kernels: 86.4 us -> 82.2 us  [sublayer(): pl.pallas_call(functools.partial(sublayer_kernel, inv_root), out_shape=(j...]
    pallas_call x0 -> x1, Pallas kernels: none -> 2.26 us  [place(): pl.pallas_call(place_kernel, out_shape=tuple((jax.ShapeDtypeStruct(a.shap...]
where the time goes in v5:
time: 85.4 us; the launch traced here: 85.1 us
  Pallas kernels  84.5 us (99%)
    pallas_call x1, Pallas kernels, sublayer(): pl.pallas_call(functools.partial(sublayer_kernel, inv_root), out_shape=(j...  82.2 us
    pallas_call x1, Pallas kernels, place(): pl.pallas_call(place_kernel, out_shape=tuple((jax.ShapeDtypeStruct(a.shap...  2.26 us

profile of v5, /device:TPU:1, one launch (start us, length us, event | category | flops | bytes accessed | tf_op | source)
XLA Modules:
  0.0 85.1 jit_solution(4343849219798290355)
XLA Ops:
  0.6 82.2 %shard_map.76 = (bf16[256,1024]{1,0:T(8,128)(2,1)}, bf16[256,1024]{1,0:T(8,128)(2,1)}, f32[8,4096]{1,0:T(8,128)}) custom-call(bf16[1024,4096]{1,0:T(8,128)(2,1)} %weights.1, bf16[256,1024]{1,0:T(8,128)(2,1)} %bitcast.6, bf16[256,1024]{1,0:T(8,128)(2,1)} %bitcast.7, s32[16,16]{1,0:T(8,128)} %bitcast.8, f32[1,1024]{1,0:T(1,128)} %bitcast.9), custom_call_target="tpu_custom_call" | custom-call | tf_op jit(solution)/shard_map/pallas_call | solution.py:638
  82.9 2.3 %shard_map.77 = (bf16[256,1024]{1,0:T(8,128)(2,1)}, bf16[256,1024]{1,0:T(8,128)(2,1)}, f32[8,4096]{1,0:T(8,128)}) custom-call(bf16[256,1024]{1,0:T(8,128)(2,1)} %get-tuple-element.9.refs_0_, bf16[256,1024]{1,0:T(8,128)(2,1)} %get-tuple-element.10.refs_1_, f32[8,4096]{1,0:T(8,128)} %get-tuple-element.11.refs_2_), custom_call_target="tpu_custom_call" | custom-call | tf_op jit(solution)/shard_map/pallas_call | solution.py:689

commit v6 on v5

--- a/solution.py
+++ b/solution.py
@@ -544,20 +544,42 @@
     ring_start(0, 0)
     start_up(3)
     finish(2)
-    ring_start(3, 0)
+    @pl.when(core == 0)
+    def _():
+        swap_wait(1)
+        ring_start(1, 0)
+
+    @pl.when(core == 1)
+    def _():
+        ring_start(3, 0)
+
     ring_relay(0, 0)
-    finish(3)
-    for c in (1, 2):
-        swap_wait(c)
-        ring_start(c, 0)
-    ring_relay(3, 0)
     flat = attended[...].reshape(256, 1024)
     for n in range(4):
         columns = slice(256 * n, 256 * n + 256)
         product = dot_nn(flat, weight_vmem[:, 3072 + 256 * n : 3328 + 256 * n])
         block_output[:, columns] = (tokens[:, columns].astype(f32) + mask[...] * product).astype(bf16)
-    ring_relay(1, 0)
-    ring_relay(2, 0)
+    finish(3)
+
+    @pl.when(core == 0)
+    def _():
+        swap_wait(2)
+        ring_start(2, 0)
+        ring_relay(1, 0)
+        ring_start(3, 0)
+        ring_relay(2, 0)
+        ring_relay(3, 0)
+
+    @pl.when(core == 1)
+    def _():
+        swap_wait(1)
+        ring_start(1, 0)
+        ring_relay(3, 0)
+        swap_wait(2)
+        ring_start(2, 0)
+        ring_relay(1, 0)
+        ring_relay(2, 0)
+
     flat = gproj[...].reshape(256, 3072)
     for n in range(4):
         rows = slice(256 * n, 256 * n + 256)

time: 85.4 us -> 85.1 us (level)
  no operation moved by 1% of the time
where the time goes in v6:
time: 85.1 us; the launch traced here: 85 us
  Pallas kernels  84.3 us (99%)
    pallas_call x1, Pallas kernels, sublayer(): pl.pallas_call(functools.partial(sublayer_kernel, inv_root), out_shape=(j...  82.1 us
    pallas_call x1, Pallas kernels, place(): pl.pallas_call(place_kernel, out_shape=tuple((jax.ShapeDtypeStruct(a.shap...  2.26 us

profile of v6, /device:TPU:1, one launch (start us, length us, event | category | flops | bytes accessed | tf_op | source)
XLA Modules:
  0.0 85.0 jit_solution(16414821395762210579)
XLA Ops:
  0.6 82.1 %shard_map.76 = (bf16[256,1024]{1,0:T(8,128)(2,1)}, bf16[256,1024]{1,0:T(8,128)(2,1)}, f32[8,4096]{1,0:T(8,128)}) custom-call(bf16[1024,4096]{1,0:T(8,128)(2,1)} %weights.1, bf16[256,1024]{1,0:T(8,128)(2,1)} %bitcast.6, bf16[256,1024]{1,0:T(8,128)(2,1)} %bitcast.7, s32[16,16]{1,0:T(8,128)} %bitcast.8, f32[1,1024]{1,0:T(1,128)} %bitcast.9), custom_call_target="tpu_custom_call" | custom-call | tf_op jit(solution)/shard_map/pallas_call | solution.py:660
  82.7 2.3 %shard_map.77 = (bf16[256,1024]{1,0:T(8,128)(2,1)}, bf16[256,1024]{1,0:T(8,128)(2,1)}, f32[8,4096]{1,0:T(8,128)}) custom-call(bf16[256,1024]{1,0:T(8,128)(2,1)} %get-tuple-element.9.refs_0_, bf16[256,1024]{1,0:T(8,128)(2,1)} %get-tuple-element.10.refs_1_, f32[8,4096]{1,0:T(8,128)} %get-tuple-element.11.refs_2_), custom_call_target="tpu_custom_call" | custom-call | tf_op jit(solution)/shard_map/pallas_call | solution.py:711
